TPU v7x, 32 devices: a whole 2x2x4 slice. The times are simulated.
32 devices in a mesh: grp: 8 (over z, core), reg: 4 (over y, x).
Axes of the slice: x: 2, y: 2, z: 4, core: 2. Of those that a mesh axis runs over, the one named last changes fastest.
Arguments:
- queries: bfloat16 [4096, 1536], P(('grp', 'reg')), parts along dimension 0, may hold values from -9 to 9
- keys_now: bfloat16 [4096, 1536], P(('grp', 'reg')), parts along dimension 0, may hold values from -9 to 9
- values_now: bfloat16 [4096, 1536], P(('grp', 'reg')), parts along dimension 0, may hold values from -6 to 6
- keys_stale: bfloat16 [4096, 1536], P(('grp', 'reg')), parts along dimension 0, may hold values from -9 to 9
- values_stale: bfloat16 [4096, 1536], P(('grp', 'reg')), parts along dimension 0, may hold values from -6 to 6
- neighbours: int32 [32, 2], P('grp'), parts along dimension 0, may hold values from -1 to 3, as said below
Outputs:
- attended: bfloat16 [4096, 1536], P(('grp', 'reg')), parts along dimension 0
There are 8 independent parts, one for each index of `grp`. A program takes and returns all parts, laid end to end along the dimension named above; each array names one. Nothing has to cross between parts.
Inputs may be any that keep to these rules, and one draw needn't show every extreme that they name: `neighbours`: row r holds first between 1 and 2 distinct region numbers other than r, then -1 in its remaining slots; some row holds 2 numbers.
All inputs are finite; a program needn't handle non-finite values.
Results may differ from a plain program's by a relative error of at most 0.0085.
Values may be sent and summed in bfloat16 or wider, within the bound.
No kernel may reach another device: no remote copies, remote signals or barrier semaphores. Data moves between devices by JAX's collectives and lax.ppermute only.
A program may use at most 128 MiB of HBM per device.

v0:
```python
import functools
import math

import jax
import jax.numpy as jnp
from jax import lax
from jax.experimental import pallas as pl
from jax.experimental.pallas import tpu as pltpu
from jax.sharding import PartitionSpec as P


HD = 128
LANES = 128
TILE_ROWS = 16
NEVER = -1e30
VMEM_BUDGET = 2 << 20
N_CHUNKS = 4
KERNEL_VMEM = 2 << 20
SCALE2 = HD**-0.5 * math.log2(math.e)


def grid_shape(count):
    rows = max(d for d in range(1, math.isqrt(count) + 1) if count % d == 0)
    return rows, count // rows


def neighbour_of(region, shift, across, shape):
    rows, cols = shape
    y, x = region // cols, region % cols
    if across:
        return y * cols + (x + shift) % cols
    return ((y + shift) % rows) * cols + x


def pairs_of(count, shift, across, shape):
    return [(neighbour_of(d, shift, across, shape), d) for d in range(count)]


def reversed_pairs(pairs):
    return [(d, s) for s, d in pairs]


def padded(n):
    return -(-n // TILE_ROWS) * TILE_ROWS


class Chunk:
    def __init__(self, first, heads, across, visit_at):
        self.first, self.heads, self.across, self.visit_at = first, heads, across, visit_at

    def sizes(self, shape):
        rows, cols = shape
        return (rows, cols) if self.across else (cols, rows)

    def message_rows(self, rows):
        return self.heads * rows + padded(3 * self.heads)


def gather_kernel(moves, n_after, *refs):
    refs = refs[n_after:]
    n_outs = 1 + max(m[2] for m in moves)
    sources, outs, sems = refs[: -1 - n_outs], refs[-1 - n_outs : -1], refs[-1]
    copies = []
    for i, (source, start, target, layer, at, width) in enumerate(moves):
        to = outs[target] if layer is None else outs[target].at[layer]
        copies.append(
            pltpu.make_async_copy(
                sources[source].at[:, start : start + width],
                to.at[:, at : at + width],
                sems.at[i],
            )
        )
    for copy in copies:
        copy.start()
    for copy in copies:
        copy.wait()


def block_rule(chunk, count, shape, v, s, stale):
    ids = [
        (neighbour_of(d, v, not chunk.across, shape), neighbour_of(d, s, chunk.across, shape))
        for d in range(count)
    ]
    if stale:
        return False if all(q == m for q, m in ids) else True
    close = [abs(q - m) <= 1 for q, m in ids]
    if all(close):
        return None
    return [d for d in range(count) if close[d]] if any(close) else False


def blocks_of(chunks, count, shape):
    entries, rules = [], []
    for chunk in chunks:
        n_visit, n_share = chunk.sizes(shape)
        per_chunk = []
        for v in range(n_visit):
            per_visit = []
            for s in range(n_share):
                for stale in (0, 1):
                    rule = block_rule(chunk, count, shape, v, s, stale)
                    if rule is False:
                        continue
                    key = (chunk.across, v, s, stale, rule)
                    if rule is not None and key not in rules:
                        rules.append(key)
                    per_visit.append((s, stale, None if rule is None else rules.index(key)))
            per_chunk.append(per_visit)
        entries.append(per_chunk)
    return entries, rules


def table_kernel(rules, shape, listed, out):
    region = lax.axis_index("reg")
    for i, (across, v, s, stale, rule) in enumerate(rules):
        if stale:
            query_region = neighbour_of(region, v, not across, shape)
            key_region = neighbour_of(region, s, across, shape)
            hit = listed[0, query_region] == key_region
            for j in range(1, listed.shape[0]):
                hit = hit | (listed[j, query_region] == key_region)
        else:
            hit = functools.reduce(jnp.logical_or, [region == d for d in rule])
        bias = jnp.where(hit, 0.0, NEVER).astype(jnp.float32)
        out[i : i + 1, :] = jnp.full((1, LANES), bias, jnp.float32)


def attend_kernel(chunks, blocks, sizes, rows, *refs):
    refs = list(refs)
    table = refs.pop(0)
    local = {}
    for chunk, (n_visit, n_share) in zip(chunks, sizes):
        local[chunk] = (
            [refs.pop(0) for _ in range(n_visit)],
            [refs.pop(0) for _ in range(n_share)],
        )
    outs = {}
    for chunk, (n_visit, _) in zip(chunks, sizes):
        outs[chunk] = (refs.pop(0), refs.pop(0), [refs.pop(0) for _ in range(n_visit - 1)])
    lane = lax.broadcasted_iota(jnp.int32, (rows, LANES), 1)
    for chunk, plan, (n_visit, n_share) in zip(chunks, blocks, sizes):
        queries, shared = local[chunk]
        out_own, lse_own, messages = outs[chunk]
        heads = chunk.heads
        lse_all = [jnp.zeros((rows, LANES), jnp.float32) for _ in range(n_visit)]
        for h in range(heads):
            there = slice(h * HD, (h + 1) * HD)
            visiting = slice((chunk.visit_at + h) * HD, (chunk.visit_at + h + 1) * HD)
            for v in range(n_visit):
                q = queries[v][:, visiting]
                keys = jnp.concatenate([shared[s][2 * t, :, there] for s, t, _ in plan[v]], axis=0)
                values = jnp.concatenate(
                    [shared[s][2 * t + 1, :, there] for s, t, _ in plan[v]], axis=0
                )
                values = jnp.concatenate(
                    [values, jnp.ones((values.shape[0], LANES), jnp.bfloat16)], axis=1
                )
                scores = lax.dot_general(
                    q, keys, (((1,), (1,)), ((), ())), preferred_element_type=jnp.float32
                )
                pieces = []
                for i, (_, _, line) in enumerate(plan[v]):
                    piece = scores[:, i * rows : (i + 1) * rows]
                    pieces.append(piece if line is None else piece + table[line : line + 1, :])
                peak = functools.reduce(jnp.maximum, pieces).max(axis=1, keepdims=True) * SCALE2
                weights = [jnp.exp2(p * SCALE2 - peak).astype(jnp.bfloat16) for p in pieces]
                both = jnp.dot(
                    jnp.concatenate(weights, axis=1), values, preferred_element_type=jnp.float32
                )
                total = both[:, HD:]
                out = (both[:, :HD] / total).astype(jnp.bfloat16)
                lse_all[v] = jnp.where(lane == h, peak + jnp.log2(total), lse_all[v])
                if v == 0:
                    out_own[:, there] = out
                else:
                    messages[v - 1][h * rows : (h + 1) * rows, :] = out
        lse_own[...] = lse_all[0].T[: padded(heads)]
        for v in range(1, n_visit):
            flat = lse_all[v].T[: padded(heads)]
            high = flat.astype(jnp.bfloat16).astype(jnp.float32)
            middle = (flat - high).astype(jnp.bfloat16).astype(jnp.float32)
            low = flat - high - middle
            lines = [x[:heads] for x in (high, middle, low)]
            spare = padded(3 * heads) - 3 * heads
            if spare:
                lines.append(jnp.zeros((spare, rows), jnp.float32))
            messages[v - 1][heads * rows :, :] = jnp.concatenate(lines, axis=0).astype(jnp.bfloat16)


def merge_into(chunks, n_visits, rows, refs, buffer):
    first = min(c.first for c in chunks)
    at = 0
    for chunk, n_visit in zip(chunks, n_visits):
        heads = chunk.heads
        part, lse_own = refs[at], refs[at + 1]
        messages = refs[at + 2 : at + 1 + n_visit]
        at += 1 + n_visit
        flats = [lse_own[:heads]]
        for message in messages:
            lines = message[heads * rows :, :].astype(jnp.float32)
            flats.append(
                lines[:heads] + lines[heads : 2 * heads] + lines[2 * heads : 3 * heads]
            )
        top = functools.reduce(jnp.maximum, flats)
        weights = [jnp.exp2(f - top) for f in flats]
        denom = functools.reduce(jnp.add, weights)
        blank = jnp.zeros((LANES - heads, rows), jnp.float32)
        columns = [jnp.concatenate([w / denom, blank], axis=0).T for w in weights]
        for h in range(heads):
            cols = slice(h * HD, (h + 1) * HD)
            parts = [part[:, cols]] + [m[h * rows : (h + 1) * rows, :] for m in messages]
            value = functools.reduce(
                jnp.add,
                [c[:, h : h + 1] * p.astype(jnp.float32) for c, p in zip(columns, parts)],
            )
            to = chunk.first - first + h
            buffer[:, to * HD : (to + 1) * HD] = value.astype(jnp.bfloat16)


def early_merge_kernel(chunks, n_visits, rows, *refs):
    merge_into(chunks, n_visits, rows, refs[:-1], refs[-1])


def last_merge_kernel(chunks, n_visits, rows, starts, *refs):
    out, buffer, sems = refs[-3:]
    done = refs[: len(starts)]
    copies = [
        pltpu.make_async_copy(ref, out.at[:, at : at + ref.shape[1]], sems.at[i])
        for i, (ref, at) in enumerate(zip(done, starts))
    ]
    for copy in copies:
        copy.start()
    merge_into(chunks, n_visits, rows, refs[len(starts) : -3], buffer)
    first = min(c.first for c in chunks) * HD
    copies.append(
        pltpu.make_async_copy(
            buffer, out.at[:, first : first + buffer.shape[1]], sems.at[len(starts)]
        )
    )
    copies[-1].start()
    for copy in copies:
        copy.wait()


def plan_of(heads):
    half = heads // 2
    later = max(1, half // 3)
    early = half - later
    stages = []
    at = 0
    for n, visit_at in ((early, 0), (later, early)):
        if n:
            stages.append([Chunk(at, n, True, visit_at), Chunk(at + n, n, False, visit_at)])
            at += 2 * n
    return stages


def placement(resident):
    if resident:
        return (
            lambda x: pltpu.with_memory_space_constraint(x, pltpu.VMEM),
            lambda shape, dtype: pltpu.VMEM(shape, dtype),
        )
    return lambda x: x, jax.ShapeDtypeStruct


def on_device(count, queries, keys_now, values_now, keys_stale, values_stale, neighbours):
    rows, width = queries.shape
    assert rows == LANES
    shape = grid_shape(count)
    stages = plan_of(width // HD)
    chunks = [c for stage in stages for c in stage]
    assert sum(c.heads for c in chunks) * HD == width and len(chunks) == N_CHUNKS
    arriving = sum((c.sizes(shape)[1] - 1) * 4 * rows * c.heads * HD * 2 for c in chunks)
    resident = arriving <= VMEM_BUDGET
    in_vmem, result = placement(resident)
    params = pltpu.CompilerParams(vmem_limit_bytes=KERNEL_VMEM if resident else None)
    vmem = pl.BlockSpec(memory_space=pltpu.VMEM)
    in_hbm = pl.BlockSpec(memory_space=pltpu.HBM)

    def gather(moves, sources, shapes, after=()):
        return pl.pallas_call(
            functools.partial(gather_kernel, moves, len(after)),
            in_specs=[vmem if resident else in_hbm] * len(after) + [in_hbm] * len(sources),
            out_specs=[vmem] * len(shapes),
            out_shape=[result(x, jnp.bfloat16) for x in shapes],
            scratch_shapes=[pltpu.SemaphoreType.DMA((len(moves),))],
            compiler_params=params,
            name="gather",
        )(
            *[in_vmem(x) for x in after],
            *[pltpu.with_memory_space_constraint(x, pltpu.HBM) for x in sources],
        )

    by_way = {way: [c for c in chunks if c.across == way] for way in (True, False)}
    moves = [
        (0, c.first * HD, int(way), None, c.visit_at * HD, c.heads * HD)
        for way in (True, False)
        for c in by_way[way]
    ]
    widths = [sum(c.heads for c in by_way[bool(i)]) * HD for i in range(2)]
    mine = gather(moves, [queries], [(rows, w) for w in widths])
    visiting = {}
    for way in (False, True):
        visiting[way] = [mine[int(way)]] + [
            lax.ppermute(mine[int(way)], "reg", pairs_of(count, v, not way, shape))
            for v in range(1, by_way[way][0].sizes(shape)[0])
        ]
    moves = [
        (a, c.first * HD, i, a, 0, c.heads * HD) for i, c in enumerate(chunks) for a in range(4)
    ]
    packed = gather(
        moves,
        [keys_now, values_now, keys_stale, values_stale],
        [(4, rows, c.heads * HD) for c in chunks],
        after=mine,
    )
    shared = {}
    for chunk, pack in zip(chunks, packed):
        shared[chunk] = [pack] + [
            lax.ppermute(pack, "reg", pairs_of(count, s, chunk.across, shape))
            for s in range(1, chunk.sizes(shape)[1])
        ]

    blocks, rules = blocks_of(chunks, count, shape)
    blocks = dict(zip(chunks, blocks))
    table = pl.pallas_call(
        functools.partial(table_kernel, rules, shape),
        in_specs=[pl.BlockSpec(memory_space=pltpu.SMEM)],
        out_specs=vmem,
        out_shape=result((padded(len(rules)), LANES), jnp.float32),
        compiler_params=params,
            name="table",
    )(neighbours.T)

    results = {}
    for stage in [[c] for c in chunks]:
        sizes = [c.sizes(shape) for c in stage]
        operands = [table]
        for chunk in stage:
            operands += visiting[chunk.across] + shared[chunk]
        out_shape = []
        for chunk, (n_visit, _) in zip(stage, sizes):
            out_shape += [
                result((rows, chunk.heads * HD), jnp.bfloat16),
                result((padded(chunk.heads), rows), jnp.float32),
            ]
            out_shape += [result((chunk.message_rows(rows), HD), jnp.bfloat16)] * (n_visit - 1)
        outs = pl.pallas_call(
            functools.partial(attend_kernel, stage, [blocks[c] for c in stage], sizes, rows),
            in_specs=[vmem] * len(operands),
            out_specs=[vmem] * len(out_shape),
            out_shape=out_shape,
            compiler_params=params,
            name="attend",
        )(*[in_vmem(x) for x in operands])
        outs = list(outs)
        for chunk, (n_visit, _) in zip(stage, sizes):
            kept = [outs.pop(0), outs.pop(0)]
            for v in range(1, n_visit):
                pairs = reversed_pairs(pairs_of(count, v, not chunk.across, shape))
                kept.append(lax.ppermute(outs.pop(0), "reg", pairs))
            results[chunk] = [in_vmem(x) for x in kept]

    merged, starts = [], []
    for stage in stages[:-1]:
        operands = [x for c in stage for x in results[c]]
        merged.append(
            pl.pallas_call(
                functools.partial(
                    early_merge_kernel, stage, [c.sizes(shape)[0] for c in stage], rows
                ),
                in_specs=[vmem] * len(operands),
                out_specs=vmem,
                out_shape=result((rows, sum(c.heads for c in stage) * HD), jnp.bfloat16),
                compiler_params=params,
            name="merge",
            )(*operands)
        )
        starts.append(min(c.first for c in stage) * HD)
    stage = stages[-1]
    operands = [x for c in stage for x in results[c]]
    return pl.pallas_call(
        functools.partial(
            last_merge_kernel, stage, [c.sizes(shape)[0] for c in stage], rows, starts
        ),
        in_specs=[vmem] * (len(merged) + len(operands)),
        out_specs=in_hbm,
        out_shape=jax.ShapeDtypeStruct((rows, width), jnp.bfloat16),
        scratch_shapes=[
            pltpu.VMEM((rows, sum(c.heads for c in stage) * HD), jnp.bfloat16),
            pltpu.SemaphoreType.DMA((len(stages),)),
        ],
        compiler_params=params,
            name="finish",
    )(*[in_vmem(x) for x in merged], *operands)


def solution(mesh):
    in_specs = (
        P(("grp", "reg"), None),
        P(("grp", "reg"), None),
        P(("grp", "reg"), None),
        P(("grp", "reg"), None),
        P(("grp", "reg"), None),
        P("grp", None),
    )
    out_specs = P(("grp", "reg"), None)

    def step(*args):
        return on_device(mesh.shape["reg"], *args)

    return jax.shard_map(
        step, mesh=mesh, in_specs=in_specs, out_specs=out_specs, check_vma=False
    )
```

profile of v0, /device:TPU:0, one launch (start us, length us, event | category | flops | bytes accessed | tf_op | source)
XLA Modules:
  0.0 38.8 jit_solution(5804485475166096445)
XLA Ops:
  0.0 1.0 %gather.2 = (bf16[128,768]{1,0:T(8,128)(2,1)S(1)}, bf16[128,768]{1,0:T(8,128)(2,1)S(1)}) custom-call(bf16[128,1536]{1,0:T(8,128)(2,1)} %refs_0_.1), custom_call_target="tpu_custom_call" | custom-call | tf_op jit(solution)/shard_map/gather/pallas_call | solution.py:282
  1.0 1.5 %gather.3 = (bf16[4,128,512]{2,1,0:T(8,128)(2,1)S(1)}, bf16[4,128,512]{2,1,0:T(8,128)(2,1)S(1)}, bf16[4,128,256]{2,1,0:T(8,128)(2,1)S(1)}, bf16[4,128,256]{2,1,0:T(8,128)(2,1)S(1)}) custom-call(bf16[128,768]{1,0:T(8,128)(2,1)S(1)} %get-tuple-element.24.refs_0_.refs_1_, bf16[128,768]{1,0:T(8,128)(2,1)S(1)} %get-tuple-element.23.refs_1_, ...), custom_call_target="tpu_custom_call" | custom-call | tf_op jit(solution)/shard_map/gather/pallas_call | solution.py:282
  2.6 3.0 %collective-permute-start.1 = (bf16[4,128,512]{2,1,0:T(8,128)(2,1)S(1)}, bf16[4,128,512]{2,1,0:T(8,128)(2,1)S(1)}, u32[]{:S(2)}, u32[]{:S(2)}) collective-permute-start(bf16[4,128,512]{2,1,0:T(8,128)(2,1)S(1)} %get-tuple-element.25.refs_3_), channel_id=1, source_target_pairs={{1,0},{0,1},{3,2},{2,3},{5,4},{4,5},{7,6},{6,7},{9,8},{8,9},{11,10... | collective-permute-start | bytes 1572872 | tf_op jit(solution)/shard_map/ppermute | solution.py:321
  5.6 1.5 %collective-permute-start.4 = (bf16[4,128,512]{2,1,0:T(8,128)(2,1)S(1)}, bf16[4,128,512]{2,1,0:T(8,128)(2,1)S(1)}, u32[]{:S(2)}, u32[]{:S(2)}) collective-permute-start(bf16[4,128,512]{2,1,0:T(8,128)(2,1)S(1)} %get-tuple-element.29.refs_3_), channel_id=1, source_target_pairs={{2,0},{3,1},{0,2},{1,3},{6,4},{7,5},{4,6},{5,7},{10,8},{11,9},{8,1... | collective-permute-start | bytes 1572872 | tf_op jit(solution)/shard_map/ppermute | solution.py:321
  7.2 0.5 %collective-permute-start = (bf16[128,768]{1,0:T(8,128)(2,1)S(1)}, bf16[128,768]{1,0:T(8,128)(2,1)S(1)}, u32[]{:S(2)}, u32[]{:S(2)}) collective-permute-start(bf16[128,768]{1,0:T(8,128)(2,1)S(1)} %get-tuple-element.23.refs_1_), channel_id=1, source_target_pairs={{2,0},{3,1},{0,2},{1,3},{6,4},{7,5},{4,6},{5,7},{10,8},{11,9},{8,1... | collective-permute-start | bytes 589832 | tf_op jit(solution)/shard_map/ppermute | solution.py:306
  7.7 0.1 collective-permute-start.3
  7.7 1.9 %collective-permute-start.6 = (bf16[4,128,256]{2,1,0:T(8,128)(2,1)S(1)}, bf16[4,128,256]{2,1,0:T(8,128)(2,1)S(1)}, u32[]{:S(2)}, u32[]{:S(2)}) collective-permute-start(bf16[4,128,256]{2,1,0:T(8,128)(2,1)S(1)} %get-tuple-element.33.refs_3_), channel_id=1, source_target_pairs={{1,0},{0,1},{3,2},{2,3},{5,4},{4,5},{7,6},{6,7},{9,8},{8,9},{11,10... | collective-permute-start | bytes 786440 | tf_op jit(solution)/shard_map/ppermute | solution.py:321
  9.7 13.5 %collective-permute-done.refs_2_ = bf16[128,768]{1,0:T(8,128)(2,1)S(1)} collective-permute-done((bf16[128,768]{1,0:T(8,128)(2,1)S(1)}, bf16[128,768]{1,0:T(8,128)(2,1)S(1)}, u32[]{:S(2)}, u32[]{:S(2)}) %collective-permute-start) | collective-permute-done | bytes 196640 | tf_op jit(solution)/shard_map/ppermute | solution.py:306
  23.2 0.0 copy-start
  23.2 1.5 %collective-permute-start.8 = (bf16[4,128,256]{2,1,0:T(8,128)(2,1)S(1)}, bf16[4,128,256]{2,1,0:T(8,128)(2,1)S(1)}, u32[]{:S(2)}, u32[]{:S(2)}) collective-permute-start(bf16[4,128,256]{2,1,0:T(8,128)(2,1)S(1)} %get-tuple-element.37.refs_3_), channel_id=1, source_target_pairs={{2,0},{3,1},{0,2},{1,3},{6,4},{7,5},{4,6},{5,7},{10,8},{11,9},{8,1... | collective-permute-start | bytes 786440 | tf_op jit(solution)/shard_map/ppermute | solution.py:321
  24.8 0.0 copy-done
  24.8 0.6 %table.1.refs_0_ = f32[16,128]{1,0:T(8,128)S(1)} custom-call(s32[2,4]{1,0:T(2,128)S(1)} %bitcast.1), custom_call_target="tpu_custom_call" | custom-call | tf_op jit(solution)/shard_map/table/pallas_call | solution.py:327
  25.4 0.0 collective-permute-done.1.refs_4_
  25.4 1.0 %attend.4 = (bf16[128,512]{1,0:T(8,128)(2,1)S(1)}, f32[16,128]{1,0:T(8,128)S(1)}, bf16[528,128]{1,0:T(8,128)(2,1)S(1)}) custom-call(f32[16,128]{1,0:T(8,128)S(1)} %table.1.refs_0_, bf16[128,768]{1,0:T(8,128)(2,1)S(1)} %get-tuple-element.23.refs_1_, bf16[128,768]{1,0:T(8,128)(2,1)S(1)} %collective-permute-done.refs_2_, ...), custom_call_target="tpu_custom_call" | custom-call | tf_op jit(solution)/shard_map/attend/pallas_call | solution.py:349
  26.4 0.7 %collective-permute-start.2 = (bf16[528,128]{1,0:T(8,128)(2,1)S(1)}, bf16[528,128]{1,0:T(8,128)(2,1)S(1)}, u32[]{:S(2)}, u32[]{:S(2)}) collective-permute-start(bf16[528,128]{1,0:T(8,128)(2,1)S(1)} %get-tuple-element.28), channel_id=1, source_target_pairs={{0,2},{1,3},{2,0},{3,1},{4,6},{5,7},{6,4},{7,5},{8,10},{9,11},{10,... | collective-permute-start | bytes 405512 | tf_op jit(solution)/shard_map/ppermute | solution.py:362
  27.1 0.0 collective-permute-done.3.refs_2_
  27.1 0.0 collective-permute-done.4.refs_4_
  27.1 1.6 %attend.5 = (bf16[128,512]{1,0:T(8,128)(2,1)S(1)}, f32[16,128]{1,0:T(8,128)S(1)}, bf16[528,128]{1,0:T(8,128)(2,1)S(1)}) custom-call(f32[16,128]{1,0:T(8,128)S(1)} %table.1.refs_0_, bf16[128,768]{1,0:T(8,128)(2,1)S(1)} %get-tuple-element.24.refs_0_.refs_1_, bf16[128,768]{1,0:T(8,128)(2,1)S(1)} %collective-permute-done.3.refs_2_, ...), custom_call_target="tpu_custom_call" | custom-call | tf_op jit(solution)/shard_map/attend/pallas_call | solution.py:349
  28.7 0.6 %collective-permute-start.5 = (bf16[528,128]{1,0:T(8,128)(2,1)S(1)}, bf16[528,128]{1,0:T(8,128)(2,1)S(1)}, u32[]{:S(2)}, u32[]{:S(2)}) collective-permute-start(bf16[528,128]{1,0:T(8,128)(2,1)S(1)} %get-tuple-element.32), channel_id=1, source_target_pairs={{0,1},{1,0},{2,3},{3,2},{4,5},{5,4},{6,7},{7,6},{8,9},{9,8},{10,11... | collective-permute-start | bytes 405512 | tf_op jit(solution)/shard_map/ppermute | solution.py:362
  29.3 0.0 collective-permute-done.6.refs_4_
  29.3 0.7 %attend.6 = (bf16[128,256]{1,0:T(8,128)(2,1)S(1)}, f32[16,128]{1,0:T(8,128)S(1)}, bf16[272,128]{1,0:T(8,128)(2,1)S(1)}) custom-call(f32[16,128]{1,0:T(8,128)S(1)} %table.1.refs_0_, bf16[128,768]{1,0:T(8,128)(2,1)S(1)} %get-tuple-element.23.refs_1_, bf16[128,768]{1,0:T(8,128)(2,1)S(1)} %collective-permute-done.refs_2_, ...), custom_call_target="tpu_custom_call" | custom-call | tf_op jit(solution)/shard_map/attend/pallas_call | solution.py:349
  30.0 1.4 %collective-permute-start.7 = (bf16[272,128]{1,0:T(8,128)(2,1)S(1)}, bf16[272,128]{1,0:T(8,128)(2,1)S(1)}, u32[]{:S(2)}, u32[]{:S(2)}) collective-permute-start(bf16[272,128]{1,0:T(8,128)(2,1)S(1)} %get-tuple-element.36), channel_id=1, source_target_pairs={{0,2},{1,3},{2,0},{3,1},{4,6},{5,7},{6,4},{7,5},{8,10},{9,11},{10,... | collective-permute-start | bytes 208904 | tf_op jit(solution)/shard_map/ppermute | solution.py:362
  31.4 0.9 %collective-permute-done.8.refs_4_ = bf16[4,128,256]{2,1,0:T(8,128)(2,1)S(1)} collective-permute-done((bf16[4,128,256]{2,1,0:T(8,128)(2,1)S(1)}, bf16[4,128,256]{2,1,0:T(8,128)(2,1)S(1)}, u32[]{:S(2)}, u32[]{:S(2)}) %collective-permute-start.8) | collective-permute-done | bytes 262176 | tf_op jit(solution)/shard_map/ppermute | solution.py:321
  32.3 1.0 %attend.7 = (bf16[128,256]{1,0:T(8,128)(2,1)S(1)}, f32[16,128]{1,0:T(8,128)S(1)}, bf16[272,128]{1,0:T(8,128)(2,1)S(1)}) custom-call(f32[16,128]{1,0:T(8,128)S(1)} %table.1.refs_0_, bf16[128,768]{1,0:T(8,128)(2,1)S(1)} %get-tuple-element.24.refs_0_.refs_1_, bf16[128,768]{1,0:T(8,128)(2,1)S(1)} %collective-permute-done.3.refs_2_, ...), custom_call_target="tpu_custom_call" | custom-call | tf_op jit(solution)/shard_map/attend/pallas_call | solution.py:349
  33.3 0.6 %collective-permute-start.9 = (bf16[272,128]{1,0:T(8,128)(2,1)S(1)}, bf16[272,128]{1,0:T(8,128)(2,1)S(1)}, u32[]{:S(2)}, u32[]{:S(2)}) collective-permute-start(bf16[272,128]{1,0:T(8,128)(2,1)S(1)} %get-tuple-element.40), channel_id=1, source_target_pairs={{0,1},{1,0},{2,3},{3,2},{4,5},{5,4},{6,7},{7,6},{8,9},{9,8},{10,11... | collective-permute-start | bytes 208904 | tf_op jit(solution)/shard_map/ppermute | solution.py:362
  33.9 0.0 collective-permute-done.2.refs_2_
  33.9 0.6 %collective-permute-done.5.refs_5_ = bf16[528,128]{1,0:T(8,128)(2,1)S(1)} collective-permute-done((bf16[528,128]{1,0:T(8,128)(2,1)S(1)}, bf16[528,128]{1,0:T(8,128)(2,1)S(1)}, u32[]{:S(2)}, u32[]{:S(2)}) %collective-permute-start.5) | collective-permute-done | bytes 135200 | tf_op jit(solution)/shard_map/ppermute | solution.py:362
  34.5 0.6 %merge.1.refs_0_ = bf16[128,1024]{1,0:T(8,128)(2,1)S(1)} custom-call(bf16[128,512]{1,0:T(8,128)(2,1)S(1)} %get-tuple-element.26.refs_0_, f32[16,128]{1,0:T(8,128)S(1)} %get-tuple-element.27.refs_1_, bf16[528,128]{1,0:T(8,128)(2,1)S(1)} %collective-permute-done.2.refs_2_, bf16[128,512]{1,0:T(8,128)(2,1)S(1)} %get-tuple-element.30.refs_3_, ...), custom_call_target="tpu_custom_call" | custom-call | tf_op jit(solution)/shard_map/merge/pallas_call | solution.py:369
  35.1 0.0 collective-permute-done.7.refs_3_
  35.1 2.6 %collective-permute-done.9.refs_6_ = bf16[272,128]{1,0:T(8,128)(2,1)S(1)} collective-permute-done((bf16[272,128]{1,0:T(8,128)(2,1)S(1)}, bf16[272,128]{1,0:T(8,128)(2,1)S(1)}, u32[]{:S(2)}, u32[]{:S(2)}) %collective-permute-start.9) | collective-permute-done | bytes 69664 | tf_op jit(solution)/shard_map/ppermute | solution.py:362
  37.7 1.1 %finish.1 = bf16[128,1536]{1,0:T(8,128)(2,1)} custom-call(bf16[128,1024]{1,0:T(8,128)(2,1)S(1)} %merge.1.refs_0_, bf16[128,256]{1,0:T(8,128)(2,1)S(1)} %get-tuple-element.34.refs_1_, f32[16,128]{1,0:T(8,128)S(1)} %get-tuple-element.35.refs_2_, bf16[272,128]{1,0:T(8,128)(2,1)S(1)} %collective-permute-done.7.refs_3_, ...), custom_call_target="tpu_custom_call" | custom-call | tf_op jit(solution)/shard_map/finish/pallas_call | solution.py:383
Async XLA Ops:
  2.6 22.8 %collective-permute-start.1 = (bf16[4,128,512]{2,1,0:T(8,128)(2,1)S(1)}, bf16[4,128,512]{2,1,0:T(8,128)(2,1)S(1)}, u32[]{:S(2)}, u32[]{:S(2)}) collective-permute-start(bf16[4,128,512]{2,1,0:T(8,128)(2,1)S(1)} %get-tuple-element.25.refs_3_), channel_id=1, source_target_pairs={{1,0},{0,1},{3,2},{2,3},{5,4},{4,5},{7,6},{6,7},{9,8},{8,9},{11,10... | collective-permute-start | bytes 1572872 | tf_op jit(solution)/shard_map/ppermute | solution.py:321
  5.6 21.5 %collective-permute-start.4 = (bf16[4,128,512]{2,1,0:T(8,128)(2,1)S(1)}, bf16[4,128,512]{2,1,0:T(8,128)(2,1)S(1)}, u32[]{:S(2)}, u32[]{:S(2)}) collective-permute-start(bf16[4,128,512]{2,1,0:T(8,128)(2,1)S(1)} %get-tuple-element.29.refs_3_), channel_id=1, source_target_pairs={{2,0},{3,1},{0,2},{1,3},{6,4},{7,5},{4,6},{5,7},{10,8},{11,9},{8,1... | collective-permute-start | bytes 1572872 | tf_op jit(solution)/shard_map/ppermute | solution.py:321
  7.2 16.1 %collective-permute-start = (bf16[128,768]{1,0:T(8,128)(2,1)S(1)}, bf16[128,768]{1,0:T(8,128)(2,1)S(1)}, u32[]{:S(2)}, u32[]{:S(2)}) collective-permute-start(bf16[128,768]{1,0:T(8,128)(2,1)S(1)} %get-tuple-element.23.refs_1_), channel_id=1, source_target_pairs={{2,0},{3,1},{0,2},{1,3},{6,4},{7,5},{4,6},{5,7},{10,8},{11,9},{8,1... | collective-permute-start | bytes 589832 | tf_op jit(solution)/shard_map/ppermute | solution.py:306
  7.7 19.5 %collective-permute-start.3 = (bf16[128,768]{1,0:T(8,128)(2,1)S(1)}, bf16[128,768]{1,0:T(8,128)(2,1)S(1)}, u32[]{:S(2)}, u32[]{:S(2)}) collective-permute-start(bf16[128,768]{1,0:T(8,128)(2,1)S(1)} %get-tuple-element.24.refs_0_.refs_1_), channel_id=1, source_target_pairs={{1,0},{0,1},{3,2},{2,3},{5,4},{4,5},{7,6},{6,7},{9,8},{8,9},{11,10... | collective-permute-start | bytes 589832 | tf_op jit(solution)/shard_map/ppermute | solution.py:306
  7.7 21.5 %collective-permute-start.6 = (bf16[4,128,256]{2,1,0:T(8,128)(2,1)S(1)}, bf16[4,128,256]{2,1,0:T(8,128)(2,1)S(1)}, u32[]{:S(2)}, u32[]{:S(2)}) collective-permute-start(bf16[4,128,256]{2,1,0:T(8,128)(2,1)S(1)} %get-tuple-element.33.refs_3_), channel_id=1, source_target_pairs={{1,0},{0,1},{3,2},{2,3},{5,4},{4,5},{7,6},{6,7},{9,8},{8,9},{11,10... | collective-permute-start | bytes 786440 | tf_op jit(solution)/shard_map/ppermute | solution.py:321
  23.2 1.5 %copy-start = (s32[4,2]{0,1:T(2,128)S(1)}, s32[4,2]{0,1:T(2,128)}, u32[]{:S(2)}) copy-start(s32[4,2]{0,1:T(2,128)} %param.11) | copy-start | bytes 100
  23.2 9.1 %collective-permute-start.8 = (bf16[4,128,256]{2,1,0:T(8,128)(2,1)S(1)}, bf16[4,128,256]{2,1,0:T(8,128)(2,1)S(1)}, u32[]{:S(2)}, u32[]{:S(2)}) collective-permute-start(bf16[4,128,256]{2,1,0:T(8,128)(2,1)S(1)} %get-tuple-element.37.refs_3_), channel_id=1, source_target_pairs={{2,0},{3,1},{0,2},{1,3},{6,4},{7,5},{4,6},{5,7},{10,8},{11,9},{8,1... | collective-permute-start | bytes 786440 | tf_op jit(solution)/shard_map/ppermute | solution.py:321
  26.4 7.5 %collective-permute-start.2 = (bf16[528,128]{1,0:T(8,128)(2,1)S(1)}, bf16[528,128]{1,0:T(8,128)(2,1)S(1)}, u32[]{:S(2)}, u32[]{:S(2)}) collective-permute-start(bf16[528,128]{1,0:T(8,128)(2,1)S(1)} %get-tuple-element.28), channel_id=1, source_target_pairs={{0,2},{1,3},{2,0},{3,1},{4,6},{5,7},{6,4},{7,5},{8,10},{9,11},{10,... | collective-permute-start | bytes 405512 | tf_op jit(solution)/shard_map/ppermute | solution.py:362
  28.7 5.8 %collective-permute-start.5 = (bf16[528,128]{1,0:T(8,128)(2,1)S(1)}, bf16[528,128]{1,0:T(8,128)(2,1)S(1)}, u32[]{:S(2)}, u32[]{:S(2)}) collective-permute-start(bf16[528,128]{1,0:T(8,128)(2,1)S(1)} %get-tuple-element.32), channel_id=1, source_target_pairs={{0,1},{1,0},{2,3},{3,2},{4,5},{5,4},{6,7},{7,6},{8,9},{9,8},{10,11... | collective-permute-start | bytes 405512 | tf_op jit(solution)/shard_map/ppermute | solution.py:362
  30.0 5.1 %collective-permute-start.7 = (bf16[272,128]{1,0:T(8,128)(2,1)S(1)}, bf16[272,128]{1,0:T(8,128)(2,1)S(1)}, u32[]{:S(2)}, u32[]{:S(2)}) collective-permute-start(bf16[272,128]{1,0:T(8,128)(2,1)S(1)} %get-tuple-element.36), channel_id=1, source_target_pairs={{0,2},{1,3},{2,0},{3,1},{4,6},{5,7},{6,4},{7,5},{8,10},{9,11},{10,... | collective-permute-start | bytes 208904 | tf_op jit(solution)/shard_map/ppermute | solution.py:362
  33.3 4.3 %collective-permute-start.9 = (bf16[272,128]{1,0:T(8,128)(2,1)S(1)}, bf16[272,128]{1,0:T(8,128)(2,1)S(1)}, u32[]{:S(2)}, u32[]{:S(2)}) collective-permute-start(bf16[272,128]{1,0:T(8,128)(2,1)S(1)} %get-tuple-element.40), channel_id=1, source_target_pairs={{0,1},{1,0},{2,3},{3,2},{4,5},{5,4},{6,7},{7,6},{8,9},{9,8},{10,11... | collective-permute-start | bytes 208904 | tf_op jit(solution)/shard_map/ppermute | solution.py:362
where the time goes:
time: 38.9 us; the launch traced here: 38.8 us
  waiting for transfers between devices  17.7 us (46%)
  starting transfers between devices  11.8 us (30%)
  Pallas kernels  9.17 us (24%)
    ppermute x2, waiting for transfers between devices, on_device(): lax.ppermute(mine[int(way)], 'reg', pairs_of(count, v, not way, shape))  13.5 us
    ppermute x4, starting transfers between devices, on_device(): lax.ppermute(pack, 'reg', pairs_of(count, s, chunk.across, shape))  8.02 us
    pallas_call x4, Pallas kernels, on_device(): pl.pallas_call(functools.partial(attend_kernel, stage, [blocks[c] for c i...  4.34 us
    ppermute x4, starting transfers between devices, on_device(): kept.append(lax.ppermute(outs.pop(0), 'reg', pairs))  3.24 us
    ppermute x4, waiting for transfers between devices, on_device(): kept.append(lax.ppermute(outs.pop(0), 'reg', pairs))  3.2 us
    pallas_call x2, Pallas kernels, gather(): pl.pallas_call(functools.partial(gather_kernel, moves, len(after)), in_sp...  2.58 us
    pallas_call x1, Pallas kernels, on_device(): pl.pallas_call(functools.partial(last_merge_kernel, stage, [c.sizes(shape...  1.09 us
    ppermute x4, waiting for transfers between devices, on_device(): lax.ppermute(pack, 'reg', pairs_of(count, s, chunk.across, shape))  0.96 us
  transfers between devices with their start and end apart: 10, of which 4 were waited for; matrix products, arithmetic and copies ran while one was open for 0% of the time, Pallas kernels for 14%

commit v1 on v0

--- a/solution.py
+++ b/solution.py
@@ -14,7 +14,6 @@
 TILE_ROWS = 16
 NEVER = -1e30
 VMEM_BUDGET = 2 << 20
-N_CHUNKS = 4
 KERNEL_VMEM = 2 << 20
 SCALE2 = HD**-0.5 * math.log2(math.e)
 
@@ -242,16 +241,19 @@
         copy.wait()
 
 
-def plan_of(heads):
-    half = heads // 2
-    later = max(1, half // 3)
-    early = half - later
+def n_stages(count):
+    return 3 if count <= 4 else 2
+
+
+def plan_of(heads, count):
+    half, n = heads // 2, n_stages(count)
+    sizes = [half // n + (i < half % n) for i in range(n)]
     stages = []
-    at = 0
-    for n, visit_at in ((early, 0), (later, early)):
-        if n:
-            stages.append([Chunk(at, n, True, visit_at), Chunk(at + n, n, False, visit_at)])
-            at += 2 * n
+    at = visit_at = 0
+    for n in sizes:
+        stages.append([Chunk(at, n, True, visit_at), Chunk(at + n, n, False, visit_at)])
+        at += 2 * n
+        visit_at += n
     return stages
 
 
@@ -268,9 +270,9 @@
     rows, width = queries.shape
     assert rows == LANES
     shape = grid_shape(count)
-    stages = plan_of(width // HD)
+    stages = plan_of(width // HD, count)
     chunks = [c for stage in stages for c in stage]
-    assert sum(c.heads for c in chunks) * HD == width and len(chunks) == N_CHUNKS
+    assert sum(c.heads for c in chunks) * HD == width and min(c.heads for c in chunks) > 0
     arriving = sum((c.sizes(shape)[1] - 1) * 4 * rows * c.heads * HD * 2 for c in chunks)
     resident = arriving <= VMEM_BUDGET
     in_vmem, result = placement(resident)

time: 38.9 us -> 39 us (level)
  waiting for transfers between devices: 17.7 us -> 9 us
  starting transfers between devices: 11.8 us -> 19.3 us
  Pallas kernels: 9.17 us -> 10.4 us
    ppermute x2, waiting for transfers between devices: 13.5 us -> 5.82 us  [on_device(): lax.ppermute(mine[int(way)], 'reg', pairs_of(count, v, not way, shape))]
    ppermute x4 -> x6, starting transfers between devices: 3.24 us -> 7.2 us  [on_device(): kept.append(lax.ppermute(outs.pop(0), 'reg', pairs))]
    ppermute x4 -> x6, starting transfers between devices: 8.02 us -> 10.1 us  [on_device(): lax.ppermute(pack, 'reg', pairs_of(count, s, chunk.across, shape))]
    ppermute x2, starting transfers between devices: 0.58 us -> 2 us  [on_device(): lax.ppermute(mine[int(way)], 'reg', pairs_of(count, v, not way, shape))]
    pallas_call x4 -> x6, Pallas kernels: 4.34 us -> 5.15 us  [on_device(): pl.pallas_call(functools.partial(attend_kernel, stage, [blocks[c] for c i...]
    ppermute x4 -> x6, waiting for transfers between devices: 0.96 us -> 0.23 us  [on_device(): lax.ppermute(pack, 'reg', pairs_of(count, s, chunk.across, shape))]
    pallas_call x1 -> x2, Pallas kernels: 0.56 us -> 0.84 us  [on_device(): pl.pallas_call(functools.partial(early_merge_kernel, stage, [c.sizes(shap...]
    ppermute x4 -> x6, waiting for transfers between devices: 3.2 us -> 2.95 us  [on_device(): kept.append(lax.ppermute(outs.pop(0), 'reg', pairs))]
  transfers between devices with their start and end apart: 10 -> 14, of which waited for: 4 -> 5; matrix products, arithmetic and copies ran while one was open for 0% -> 0% of each run, Pallas kernels for 14% -> 17%
where the time goes in v1:
time: 39 us; the launch traced here: 38.8 us
  starting transfers between devices  19.3 us (49%)
  Pallas kernels  10.4 us (27%)
  waiting for transfers between devices  9 us (23%)
    ppermute x6, starting transfers between devices, on_device(): lax.ppermute(pack, 'reg', pairs_of(count, s, chunk.across, shape))  10.1 us
    ppermute x6, starting transfers between devices, on_device(): kept.append(lax.ppermute(outs.pop(0), 'reg', pairs))  7.2 us
    ppermute x2, waiting for transfers between devices, on_device(): lax.ppermute(mine[int(way)], 'reg', pairs_of(count, v, not way, shape))  5.82 us
    pallas_call x6, Pallas kernels, on_device(): pl.pallas_call(functools.partial(attend_kernel, stage, [blocks[c] for c i...  5.15 us
    ppermute x6, waiting for transfers between devices, on_device(): kept.append(lax.ppermute(outs.pop(0), 'reg', pairs))  2.95 us
    pallas_call x2, Pallas kernels, gather(): pl.pallas_call(functools.partial(gather_kernel, moves, len(after)), in_sp...  2.69 us
    ppermute x2, starting transfers between devices, on_device(): lax.ppermute(mine[int(way)], 'reg', pairs_of(count, v, not way, shape))  2 us
    pallas_call x1, Pallas kernels, on_device(): pl.pallas_call(functools.partial(last_merge_kernel, stage, [c.sizes(shape...  1.1 us
  transfers between devices with their start and end apart: 14, of which 5 were waited for; matrix products, arithmetic and copies ran while one was open for 0% of the time, Pallas kernels for 17%

profile of v1, /device:TPU:0, one launch (start us, length us, event | category | flops | bytes accessed | tf_op | source)
XLA Modules:
  0.0 38.8 jit_solution(16634490036077176078)
XLA Ops:
  0.0 1.1 %gather.2 = (bf16[128,768]{1,0:T(8,128)(2,1)S(1)}, bf16[128,768]{1,0:T(8,128)(2,1)S(1)}) custom-call(bf16[128,1536]{1,0:T(8,128)(2,1)} %refs_0_.1), custom_call_target="tpu_custom_call" | custom-call | tf_op jit(solution)/shard_map/gather/pallas_call | solution.py:284
  1.1 1.6 %gather.3 = (bf16[4,128,256]{2,1,0:T(8,128)(2,1)S(1)}, bf16[4,128,256]{2,1,0:T(8,128)(2,1)S(1)}, bf16[4,128,256]{2,1,0:T(8,128)(2,1)S(1)}, bf16[4,128,256]{2,1,0...) custom-call(bf16[128,768]{1,0:T(8,128)(2,1)S(1)} %get-tuple-element.32.refs_0_.refs_1_, ...), custom_call_target="tpu_custom_call" | custom-call | tf_op jit(solution)/shard_map/gather/pallas_call | solution.py:284
  2.7 3.1 %collective-permute-start.8 = (bf16[4,128,256]{2,1,0:T(8,128)(2,1)S(1)}, bf16[4,128,256]{2,1,0:T(8,128)(2,1)S(1)}, u32[]{:S(2)}, u32[]{:S(2)}) collective-permute-start(bf16[4,128,256]{2,1,0:T(8,128)(2,1)S(1)} %get-tuple-element.45.refs_3_), channel_id=1, source_target_pairs={{2,0},{3,1},{0,2},{1,3},{6,4},{7,5},{4,6},{5,7},{10,8},{11,9},{8,1... | collective-permute-start | bytes 786440 | tf_op jit(solution)/shard_map/ppermute | solution.py:323
  5.8 1.5 %collective-permute-start.3 = (bf16[128,768]{1,0:T(8,128)(2,1)S(1)}, bf16[128,768]{1,0:T(8,128)(2,1)S(1)}, u32[]{:S(2)}, u32[]{:S(2)}) collective-permute-start(bf16[128,768]{1,0:T(8,128)(2,1)S(1)} %get-tuple-element.32.refs_0_.refs_1_), channel_id=1, source_target_pairs={{1,0},{0,1},{3,2},{2,3},{5,4},{4,5},{7,6},{6,7},{9,8},{8,9},{11,10... | collective-permute-start | bytes 589832 | tf_op jit(solution)/shard_map/ppermute | solution.py:308
  7.3 0.5 %collective-permute-start = (bf16[128,768]{1,0:T(8,128)(2,1)S(1)}, bf16[128,768]{1,0:T(8,128)(2,1)S(1)}, u32[]{:S(2)}, u32[]{:S(2)}) collective-permute-start(bf16[128,768]{1,0:T(8,128)(2,1)S(1)} %get-tuple-element.31.refs_1_), channel_id=1, source_target_pairs={{2,0},{3,1},{0,2},{1,3},{6,4},{7,5},{4,6},{5,7},{10,8},{11,9},{8,1... | collective-permute-start | bytes 589832 | tf_op jit(solution)/shard_map/ppermute | solution.py:308
  7.8 0.1 collective-permute-start.6
  7.9 1.9 %collective-permute-start.4 = (bf16[4,128,256]{2,1,0:T(8,128)(2,1)S(1)}, bf16[4,128,256]{2,1,0:T(8,128)(2,1)S(1)}, u32[]{:S(2)}, u32[]{:S(2)}) collective-permute-start(bf16[4,128,256]{2,1,0:T(8,128)(2,1)S(1)} %get-tuple-element.37.refs_3_), channel_id=1, source_target_pairs={{2,0},{3,1},{0,2},{1,3},{6,4},{7,5},{4,6},{5,7},{10,8},{11,9},{8,1... | collective-permute-start | bytes 786440 | tf_op jit(solution)/shard_map/ppermute | solution.py:323
  9.8 3.7 %collective-permute-done.3.refs_2_ = bf16[128,768]{1,0:T(8,128)(2,1)S(1)} collective-permute-done((bf16[128,768]{1,0:T(8,128)(2,1)S(1)}, bf16[128,768]{1,0:T(8,128)(2,1)S(1)}, u32[]{:S(2)}, u32[]{:S(2)}) %collective-permute-start.3) | collective-permute-done | bytes 196640 | tf_op jit(solution)/shard_map/ppermute | solution.py:308
  13.5 1.5 %collective-permute-start.1 = (bf16[4,128,256]{2,1,0:T(8,128)(2,1)S(1)}, bf16[4,128,256]{2,1,0:T(8,128)(2,1)S(1)}, u32[]{:S(2)}, u32[]{:S(2)}) collective-permute-start(bf16[4,128,256]{2,1,0:T(8,128)(2,1)S(1)} %get-tuple-element.33.refs_3_), channel_id=1, source_target_pairs={{1,0},{0,1},{3,2},{2,3},{5,4},{4,5},{7,6},{6,7},{9,8},{8,9},{11,10... | collective-permute-start | bytes 786440 | tf_op jit(solution)/shard_map/ppermute | solution.py:323
  15.0 2.1 %collective-permute-done.refs_2_ = bf16[128,768]{1,0:T(8,128)(2,1)S(1)} collective-permute-done((bf16[128,768]{1,0:T(8,128)(2,1)S(1)}, bf16[128,768]{1,0:T(8,128)(2,1)S(1)}, u32[]{:S(2)}, u32[]{:S(2)}) %collective-permute-start) | collective-permute-done | bytes 196640 | tf_op jit(solution)/shard_map/ppermute | solution.py:308
  17.1 2.0 %collective-permute-start.12 = (bf16[4,128,256]{2,1,0:T(8,128)(2,1)S(1)}, bf16[4,128,256]{2,1,0:T(8,128)(2,1)S(1)}, u32[]{:S(2)}, u32[]{:S(2)}) collective-permute-start(bf16[4,128,256]{2,1,0:T(8,128)(2,1)S(1)} %get-tuple-element.53.refs_3_), channel_id=1, source_target_pairs={{2,0},{3,1},{0,2},{1,3},{6,4},{7,5},{4,6},{5,7},{10,8},{11,9},{8,1... | collective-permute-start | bytes 786440 | tf_op jit(solution)/shard_map/ppermute | solution.py:323
  19.2 0.0 collective-permute-done.8.refs_4_
  19.2 0.0 copy-start
  19.2 1.5 %collective-permute-start.10 = (bf16[4,128,256]{2,1,0:T(8,128)(2,1)S(1)}, bf16[4,128,256]{2,1,0:T(8,128)(2,1)S(1)}, u32[]{:S(2)}, u32[]{:S(2)}) collective-permute-start(bf16[4,128,256]{2,1,0:T(8,128)(2,1)S(1)} %get-tuple-element.49.refs_3_), channel_id=1, source_target_pairs={{1,0},{0,1},{3,2},{2,3},{5,4},{4,5},{7,6},{6,7},{9,8},{8,9},{11,10... | collective-permute-start | bytes 786440 | tf_op jit(solution)/shard_map/ppermute | solution.py:323
  20.7 0.0 copy-done
  20.7 0.6 %table.1.refs_0_ = f32[16,128]{1,0:T(8,128)S(1)} custom-call(s32[2,4]{1,0:T(2,128)S(1)} %bitcast.1), custom_call_target="tpu_custom_call" | custom-call | tf_op jit(solution)/shard_map/table/pallas_call | solution.py:329
  21.3 1.0 %attend.9 = (bf16[128,256]{1,0:T(8,128)(2,1)S(1)}, f32[16,128]{1,0:T(8,128)S(1)}, bf16[272,128]{1,0:T(8,128)(2,1)S(1)}) custom-call(f32[16,128]{1,0:T(8,128)S(1)} %table.1.refs_0_, bf16[128,768]{1,0:T(8,128)(2,1)S(1)} %get-tuple-element.32.refs_0_.refs_1_, bf16[128,768]{1,0:T(8,128)(2,1)S(1)} %collective-permute-done.3.refs_2_, ...), custom_call_target="tpu_custom_call" | custom-call | tf_op jit(solution)/shard_map/attend/pallas_call | solution.py:351
  22.3 0.0 collective-permute-done.6.refs_4_
  22.3 0.7 %collective-permute-start.9 = (bf16[272,128]{1,0:T(8,128)(2,1)S(1)}, bf16[272,128]{1,0:T(8,128)(2,1)S(1)}, u32[]{:S(2)}, u32[]{:S(2)}) collective-permute-start(bf16[272,128]{1,0:T(8,128)(2,1)S(1)} %get-tuple-element.48), channel_id=1, source_target_pairs={{0,1},{1,0},{2,3},{3,2},{4,5},{5,4},{6,7},{7,6},{8,9},{9,8},{10,11... | collective-permute-start | bytes 208904 | tf_op jit(solution)/shard_map/ppermute | solution.py:364
  23.0 0.7 %attend.8 = (bf16[128,256]{1,0:T(8,128)(2,1)S(1)}, f32[16,128]{1,0:T(8,128)S(1)}, bf16[272,128]{1,0:T(8,128)(2,1)S(1)}) custom-call(f32[16,128]{1,0:T(8,128)S(1)} %table.1.refs_0_, bf16[128,768]{1,0:T(8,128)(2,1)S(1)} %get-tuple-element.31.refs_1_, bf16[128,768]{1,0:T(8,128)(2,1)S(1)} %collective-permute-done.refs_2_, ...), custom_call_target="tpu_custom_call" | custom-call | tf_op jit(solution)/shard_map/attend/pallas_call | solution.py:351
  23.7 0.0 collective-permute-done.4.refs_4_
  23.7 1.0 %collective-permute-start.7 = (bf16[272,128]{1,0:T(8,128)(2,1)S(1)}, bf16[272,128]{1,0:T(8,128)(2,1)S(1)}, u32[]{:S(2)}, u32[]{:S(2)}) collective-permute-start(bf16[272,128]{1,0:T(8,128)(2,1)S(1)} %get-tuple-element.44), channel_id=1, source_target_pairs={{0,2},{1,3},{2,0},{3,1},{4,6},{5,7},{6,4},{7,5},{8,10},{9,11},{10,... | collective-permute-start | bytes 208904 | tf_op jit(solution)/shard_map/ppermute | solution.py:364
  24.8 1.0 %attend.7 = (bf16[128,256]{1,0:T(8,128)(2,1)S(1)}, f32[16,128]{1,0:T(8,128)S(1)}, bf16[272,128]{1,0:T(8,128)(2,1)S(1)}) custom-call(f32[16,128]{1,0:T(8,128)S(1)} %table.1.refs_0_, bf16[128,768]{1,0:T(8,128)(2,1)S(1)} %get-tuple-element.32.refs_0_.refs_1_, bf16[128,768]{1,0:T(8,128)(2,1)S(1)} %collective-permute-done.3.refs_2_, ...), custom_call_target="tpu_custom_call" | custom-call | tf_op jit(solution)/shard_map/attend/pallas_call | solution.py:351
  25.8 0.0 collective-permute-done.1.refs_4_
  25.8 1.6 %collective-permute-start.5 = (bf16[272,128]{1,0:T(8,128)(2,1)S(1)}, bf16[272,128]{1,0:T(8,128)(2,1)S(1)}, u32[]{:S(2)}, u32[]{:S(2)}) collective-permute-start(bf16[272,128]{1,0:T(8,128)(2,1)S(1)} %get-tuple-element.40), channel_id=1, source_target_pairs={{0,1},{1,0},{2,3},{3,2},{4,5},{5,4},{6,7},{7,6},{8,9},{9,8},{10,11... | collective-permute-start | bytes 208904 | tf_op jit(solution)/shard_map/ppermute | solution.py:364
  27.3 0.7 %attend.6 = (bf16[128,256]{1,0:T(8,128)(2,1)S(1)}, f32[16,128]{1,0:T(8,128)S(1)}, bf16[272,128]{1,0:T(8,128)(2,1)S(1)}) custom-call(f32[16,128]{1,0:T(8,128)S(1)} %table.1.refs_0_, bf16[128,768]{1,0:T(8,128)(2,1)S(1)} %get-tuple-element.31.refs_1_, bf16[128,768]{1,0:T(8,128)(2,1)S(1)} %collective-permute-done.refs_2_, ...), custom_call_target="tpu_custom_call" | custom-call | tf_op jit(solution)/shard_map/attend/pallas_call | solution.py:351
  28.1 0.2 collective-permute-done.12.refs_4_
  28.3 1.7 %collective-permute-start.2 = (bf16[272,128]{1,0:T(8,128)(2,1)S(1)}, bf16[272,128]{1,0:T(8,128)(2,1)S(1)}, u32[]{:S(2)}, u32[]{:S(2)}) collective-permute-start(bf16[272,128]{1,0:T(8,128)(2,1)S(1)} %get-tuple-element.36), channel_id=1, source_target_pairs={{0,2},{1,3},{2,0},{3,1},{4,6},{5,7},{6,4},{7,5},{8,10},{9,11},{10,... | collective-permute-start | bytes 208904 | tf_op jit(solution)/shard_map/ppermute | solution.py:364
  30.0 1.0 %attend.11 = (bf16[128,256]{1,0:T(8,128)(2,1)S(1)}, f32[16,128]{1,0:T(8,128)S(1)}, bf16[272,128]{1,0:T(8,128)(2,1)S(1)}) custom-call(f32[16,128]{1,0:T(8,128)S(1)} %table.1.refs_0_, bf16[128,768]{1,0:T(8,128)(2,1)S(1)} %get-tuple-element.32.refs_0_.refs_1_, bf16[128,768]{1,0:T(8,128)(2,1)S(1)} %collective-permute-done.3.refs_2_, ...), custom_call_target="tpu_custom_call" | custom-call | tf_op jit(solution)/shard_map/attend/pallas_call | solution.py:351
  31.0 0.0 collective-permute-done.10.refs_4_
  31.0 1.6 %collective-permute-start.13 = (bf16[272,128]{1,0:T(8,128)(2,1)S(1)}, bf16[272,128]{1,0:T(8,128)(2,1)S(1)}, u32[]{:S(2)}, u32[]{:S(2)}) collective-permute-start(bf16[272,128]{1,0:T(8,128)(2,1)S(1)} %get-tuple-element.56), channel_id=1, source_target_pairs={{0,1},{1,0},{2,3},{3,2},{4,5},{5,4},{6,7},{7,6},{8,9},{9,8},{10,11... | collective-permute-start | bytes 208904 | tf_op jit(solution)/shard_map/ppermute | solution.py:364
  32.6 0.7 %attend.10 = (bf16[128,256]{1,0:T(8,128)(2,1)S(1)}, f32[16,128]{1,0:T(8,128)S(1)}, bf16[272,128]{1,0:T(8,128)(2,1)S(1)}) custom-call(f32[16,128]{1,0:T(8,128)S(1)} %table.1.refs_0_, bf16[128,768]{1,0:T(8,128)(2,1)S(1)} %get-tuple-element.31.refs_1_, bf16[128,768]{1,0:T(8,128)(2,1)S(1)} %collective-permute-done.refs_2_, ...), custom_call_target="tpu_custom_call" | custom-call | tf_op jit(solution)/shard_map/attend/pallas_call | solution.py:351
  33.3 0.0 collective-permute-done.9.refs_5_
  33.3 0.6 %collective-permute-start.11 = (bf16[272,128]{1,0:T(8,128)(2,1)S(1)}, bf16[272,128]{1,0:T(8,128)(2,1)S(1)}, u32[]{:S(2)}, u32[]{:S(2)}) collective-permute-start(bf16[272,128]{1,0:T(8,128)(2,1)S(1)} %get-tuple-element.52), channel_id=1, source_target_pairs={{0,2},{1,3},{2,0},{3,1},{4,6},{5,7},{6,4},{7,5},{8,10},{9,11},{10,... | collective-permute-start | bytes 208904 | tf_op jit(solution)/shard_map/ppermute | solution.py:364
  33.9 0.0 collective-permute-done.7.refs_2_
  33.9 0.4 %merge.3.refs_1_ = bf16[128,512]{1,0:T(8,128)(2,1)S(1)} custom-call(bf16[128,256]{1,0:T(8,128)(2,1)S(1)} %get-tuple-element.42.refs_0_, f32[16,128]{1,0:T(8,128)S(1)} %get-tuple-element.43.refs_1_, bf16[272,128]{1,0:T(8,128)(2,1)S(1)} %collective-permute-done.7.refs_2_, bf16[128,256]{1,0:T(8,128)(2,1)S(1)} %get-tuple-element.46.refs_3_, ...), custom_call_target="tpu_custom_call" | custom-call | tf_op jit(solution)/shard_map/merge/pallas_call | solution.py:371
  34.3 0.0 collective-permute-done.5.refs_5_
  34.3 0.0 collective-permute-done.2.refs_2_
  34.3 0.4 %merge.2.refs_0_ = bf16[128,512]{1,0:T(8,128)(2,1)S(1)} custom-call(bf16[128,256]{1,0:T(8,128)(2,1)S(1)} %get-tuple-element.34.refs_0_, f32[16,128]{1,0:T(8,128)S(1)} %get-tuple-element.35.refs_1_, bf16[272,128]{1,0:T(8,128)(2,1)S(1)} %collective-permute-done.2.refs_2_, bf16[128,256]{1,0:T(8,128)(2,1)S(1)} %get-tuple-element.38.refs_3_, ...), custom_call_target="tpu_custom_call" | custom-call | tf_op jit(solution)/shard_map/merge/pallas_call | solution.py:371
  34.7 0.6 %collective-permute-done.13.refs_7_ = bf16[272,128]{1,0:T(8,128)(2,1)S(1)} collective-permute-done((bf16[272,128]{1,0:T(8,128)(2,1)S(1)}, bf16[272,128]{1,0:T(8,128)(2,1)S(1)}, u32[]{:S(2)}, u32[]{:S(2)}) %collective-permute-start.13) | collective-permute-done | bytes 69664 | tf_op jit(solution)/shard_map/ppermute | solution.py:364
  35.4 2.3 %collective-permute-done.11.refs_4_ = bf16[272,128]{1,0:T(8,128)(2,1)S(1)} collective-permute-done((bf16[272,128]{1,0:T(8,128)(2,1)S(1)}, bf16[272,128]{1,0:T(8,128)(2,1)S(1)}, u32[]{:S(2)}, u32[]{:S(2)}) %collective-permute-start.11) | collective-permute-done | bytes 69664 | tf_op jit(solution)/shard_map/ppermute | solution.py:364
  37.7 1.1 %finish.1 = bf16[128,1536]{1,0:T(8,128)(2,1)} custom-call(bf16[128,512]{1,0:T(8,128)(2,1)S(1)} %merge.2.refs_0_, bf16[128,512]{1,0:T(8,128)(2,1)S(1)} %merge.3.refs_1_, bf16[128,256]{1,0:T(8,128)(2,1)S(1)} %get-tuple-element.50.refs_2_, f32[16,128]{1,0:T(8,128)S(1)} %get-tuple-element.51.refs_3_, bf16[272,128]{1,0:T(8,128)(2,1)S(1)} %collective-permute-done.11.refs_4_, ...), custom_call_target="tpu_custom_call" | custom-call | tf_op jit(solution)/shard_map/finish/pallas_call | solution.py:385
Async XLA Ops:
  2.7 16.5 %collective-permute-start.8 = (bf16[4,128,256]{2,1,0:T(8,128)(2,1)S(1)}, bf16[4,128,256]{2,1,0:T(8,128)(2,1)S(1)}, u32[]{:S(2)}, u32[]{:S(2)}) collective-permute-start(bf16[4,128,256]{2,1,0:T(8,128)(2,1)S(1)} %get-tuple-element.45.refs_3_), channel_id=1, source_target_pairs={{2,0},{3,1},{0,2},{1,3},{6,4},{7,5},{4,6},{5,7},{10,8},{11,9},{8,1... | collective-permute-start | bytes 786440 | tf_op jit(solution)/shard_map/ppermute | solution.py:323
  5.8 7.8 %collective-permute-start.3 = (bf16[128,768]{1,0:T(8,128)(2,1)S(1)}, bf16[128,768]{1,0:T(8,128)(2,1)S(1)}, u32[]{:S(2)}, u32[]{:S(2)}) collective-permute-start(bf16[128,768]{1,0:T(8,128)(2,1)S(1)} %get-tuple-element.32.refs_0_.refs_1_), channel_id=1, source_target_pairs={{1,0},{0,1},{3,2},{2,3},{5,4},{4,5},{7,6},{6,7},{9,8},{8,9},{11,10... | collective-permute-start | bytes 589832 | tf_op jit(solution)/shard_map/ppermute | solution.py:308
  7.3 9.9 %collective-permute-start = (bf16[128,768]{1,0:T(8,128)(2,1)S(1)}, bf16[128,768]{1,0:T(8,128)(2,1)S(1)}, u32[]{:S(2)}, u32[]{:S(2)}) collective-permute-start(bf16[128,768]{1,0:T(8,128)(2,1)S(1)} %get-tuple-element.31.refs_1_), channel_id=1, source_target_pairs={{2,0},{3,1},{0,2},{1,3},{6,4},{7,5},{4,6},{5,7},{10,8},{11,9},{8,1... | collective-permute-start | bytes 589832 | tf_op jit(solution)/shard_map/ppermute | solution.py:308
  7.8 14.5 %collective-permute-start.6 = (bf16[4,128,256]{2,1,0:T(8,128)(2,1)S(1)}, bf16[4,128,256]{2,1,0:T(8,128)(2,1)S(1)}, u32[]{:S(2)}, u32[]{:S(2)}) collective-permute-start(bf16[4,128,256]{2,1,0:T(8,128)(2,1)S(1)} %get-tuple-element.41.refs_3_), channel_id=1, source_target_pairs={{1,0},{0,1},{3,2},{2,3},{5,4},{4,5},{7,6},{6,7},{9,8},{8,9},{11,10... | collective-permute-start | bytes 786440 | tf_op jit(solution)/shard_map/ppermute | solution.py:323
  7.9 15.9 %collective-permute-start.4 = (bf16[4,128,256]{2,1,0:T(8,128)(2,1)S(1)}, bf16[4,128,256]{2,1,0:T(8,128)(2,1)S(1)}, u32[]{:S(2)}, u32[]{:S(2)}) collective-permute-start(bf16[4,128,256]{2,1,0:T(8,128)(2,1)S(1)} %get-tuple-element.37.refs_3_), channel_id=1, source_target_pairs={{2,0},{3,1},{0,2},{1,3},{6,4},{7,5},{4,6},{5,7},{10,8},{11,9},{8,1... | collective-permute-start | bytes 786440 | tf_op jit(solution)/shard_map/ppermute | solution.py:323
  13.5 12.2 %collective-permute-start.1 = (bf16[4,128,256]{2,1,0:T(8,128)(2,1)S(1)}, bf16[4,128,256]{2,1,0:T(8,128)(2,1)S(1)}, u32[]{:S(2)}, u32[]{:S(2)}) collective-permute-start(bf16[4,128,256]{2,1,0:T(8,128)(2,1)S(1)} %get-tuple-element.33.refs_3_), channel_id=1, source_target_pairs={{1,0},{0,1},{3,2},{2,3},{5,4},{4,5},{7,6},{6,7},{9,8},{8,9},{11,10... | collective-permute-start | bytes 786440 | tf_op jit(solution)/shard_map/ppermute | solution.py:323
  17.1 11.1 %collective-permute-start.12 = (bf16[4,128,256]{2,1,0:T(8,128)(2,1)S(1)}, bf16[4,128,256]{2,1,0:T(8,128)(2,1)S(1)}, u32[]{:S(2)}, u32[]{:S(2)}) collective-permute-start(bf16[4,128,256]{2,1,0:T(8,128)(2,1)S(1)} %get-tuple-element.53.refs_3_), channel_id=1, source_target_pairs={{2,0},{3,1},{0,2},{1,3},{6,4},{7,5},{4,6},{5,7},{10,8},{11,9},{8,1... | collective-permute-start | bytes 786440 | tf_op jit(solution)/shard_map/ppermute | solution.py:323
  19.2 1.5 %copy-start = (s32[4,2]{0,1:T(2,128)S(1)}, s32[4,2]{0,1:T(2,128)}, u32[]{:S(2)}) copy-start(s32[4,2]{0,1:T(2,128)} %param.11) | copy-start | bytes 100
  19.2 11.8 %collective-permute-start.10 = (bf16[4,128,256]{2,1,0:T(8,128)(2,1)S(1)}, bf16[4,128,256]{2,1,0:T(8,128)(2,1)S(1)}, u32[]{:S(2)}, u32[]{:S(2)}) collective-permute-start(bf16[4,128,256]{2,1,0:T(8,128)(2,1)S(1)} %get-tuple-element.49.refs_3_), channel_id=1, source_target_pairs={{1,0},{0,1},{3,2},{2,3},{5,4},{4,5},{7,6},{6,7},{9,8},{8,9},{11,10... | collective-permute-start | bytes 786440 | tf_op jit(solution)/shard_map/ppermute | solution.py:323
  22.3 11.0 %collective-permute-start.9 = (bf16[272,128]{1,0:T(8,128)(2,1)S(1)}, bf16[272,128]{1,0:T(8,128)(2,1)S(1)}, u32[]{:S(2)}, u32[]{:S(2)}) collective-permute-start(bf16[272,128]{1,0:T(8,128)(2,1)S(1)} %get-tuple-element.48), channel_id=1, source_target_pairs={{0,1},{1,0},{2,3},{3,2},{4,5},{5,4},{6,7},{7,6},{8,9},{9,8},{10,11... | collective-permute-start | bytes 208904 | tf_op jit(solution)/shard_map/ppermute | solution.py:364
  23.7 10.1 %collective-permute-start.7 = (bf16[272,128]{1,0:T(8,128)(2,1)S(1)}, bf16[272,128]{1,0:T(8,128)(2,1)S(1)}, u32[]{:S(2)}, u32[]{:S(2)}) collective-permute-start(bf16[272,128]{1,0:T(8,128)(2,1)S(1)} %get-tuple-element.44), channel_id=1, source_target_pairs={{0,2},{1,3},{2,0},{3,1},{4,6},{5,7},{6,4},{7,5},{8,10},{9,11},{10,... | collective-permute-start | bytes 208904 | tf_op jit(solution)/shard_map/ppermute | solution.py:364
  25.8 8.5 %collective-permute-start.5 = (bf16[272,128]{1,0:T(8,128)(2,1)S(1)}, bf16[272,128]{1,0:T(8,128)(2,1)S(1)}, u32[]{:S(2)}, u32[]{:S(2)}) collective-permute-start(bf16[272,128]{1,0:T(8,128)(2,1)S(1)} %get-tuple-element.40), channel_id=1, source_target_pairs={{0,1},{1,0},{2,3},{3,2},{4,5},{5,4},{6,7},{7,6},{8,9},{9,8},{10,11... | collective-permute-start | bytes 208904 | tf_op jit(solution)/shard_map/ppermute | solution.py:364
  28.3 6.0 %collective-permute-start.2 = (bf16[272,128]{1,0:T(8,128)(2,1)S(1)}, bf16[272,128]{1,0:T(8,128)(2,1)S(1)}, u32[]{:S(2)}, u32[]{:S(2)}) collective-permute-start(bf16[272,128]{1,0:T(8,128)(2,1)S(1)} %get-tuple-element.36), channel_id=1, source_target_pairs={{0,2},{1,3},{2,0},{3,1},{4,6},{5,7},{6,4},{7,5},{8,10},{9,11},{10,... | collective-permute-start | bytes 208904 | tf_op jit(solution)/shard_map/ppermute | solution.py:364
  31.0 4.4 %collective-permute-start.13 = (bf16[272,128]{1,0:T(8,128)(2,1)S(1)}, bf16[272,128]{1,0:T(8,128)(2,1)S(1)}, u32[]{:S(2)}, u32[]{:S(2)}) collective-permute-start(bf16[272,128]{1,0:T(8,128)(2,1)S(1)} %get-tuple-element.56), channel_id=1, source_target_pairs={{0,1},{1,0},{2,3},{3,2},{4,5},{5,4},{6,7},{7,6},{8,9},{9,8},{10,11... | collective-permute-start | bytes 208904 | tf_op jit(solution)/shard_map/ppermute | solution.py:364
  33.3 4.4 %collective-permute-start.11 = (bf16[272,128]{1,0:T(8,128)(2,1)S(1)}, bf16[272,128]{1,0:T(8,128)(2,1)S(1)}, u32[]{:S(2)}, u32[]{:S(2)}) collective-permute-start(bf16[272,128]{1,0:T(8,128)(2,1)S(1)} %get-tuple-element.52), channel_id=1, source_target_pairs={{0,2},{1,3},{2,0},{3,1},{4,6},{5,7},{6,4},{7,5},{8,10},{9,11},{10,... | collective-permute-start | bytes 208904 | tf_op jit(solution)/shard_map/ppermute | solution.py:364

commit v2 on v1

--- a/solution.py
+++ b/solution.py
@@ -155,20 +155,24 @@
                     [values, jnp.ones((values.shape[0], LANES), jnp.bfloat16)], axis=1
                 )
                 scores = lax.dot_general(
-                    q, keys, (((1,), (1,)), ((), ())), preferred_element_type=jnp.float32
+                    keys, q, (((1,), (1,)), ((), ())), preferred_element_type=jnp.float32
                 )
                 pieces = []
                 for i, (_, _, line) in enumerate(plan[v]):
-                    piece = scores[:, i * rows : (i + 1) * rows]
+                    piece = scores[i * rows : (i + 1) * rows]
                     pieces.append(piece if line is None else piece + table[line : line + 1, :])
-                peak = functools.reduce(jnp.maximum, pieces).max(axis=1, keepdims=True) * SCALE2
+                peak = functools.reduce(jnp.maximum, pieces).max(axis=0, keepdims=True) * SCALE2
                 weights = [jnp.exp2(p * SCALE2 - peak).astype(jnp.bfloat16) for p in pieces]
-                both = jnp.dot(
-                    jnp.concatenate(weights, axis=1), values, preferred_element_type=jnp.float32
+                both = lax.dot_general(
+                    jnp.concatenate(weights, axis=0),
+                    values,
+                    (((0,), (0,)), ((), ())),
+                    preferred_element_type=jnp.float32,
                 )
                 total = both[:, HD:]
                 out = (both[:, :HD] / total).astype(jnp.bfloat16)
-                lse_all[v] = jnp.where(lane == h, peak + jnp.log2(total), lse_all[v])
+                column = jnp.broadcast_to(peak, (LANES, rows)).T
+                lse_all[v] = jnp.where(lane == h, column + jnp.log2(total), lse_all[v])
                 if v == 0:
                     out_own[:, there] = out
                 else:
@@ -294,29 +298,39 @@
             *[pltpu.with_memory_space_constraint(x, pltpu.HBM) for x in sources],
         )
 
-    by_way = {way: [c for c in chunks if c.across == way] for way in (True, False)}
+    by_way = {way: [c for c in chunks if c.across == way] for way in (False, True)}
+    first, rest = stages[0], [c for stage in stages[1:] for c in stage]
+    keyed = [keys_now, values_now, keys_stale, values_stale]
+
+    def key_moves(some, at, source):
+        return [
+            (source + a, c.first * HD, at + i, a, 0, c.heads * HD)
+            for i, c in enumerate(some)
+            for a in range(4)
+        ]
+
+    def key_shapes(some):
+        return [(4, rows, c.heads * HD) for c in some]
+
     moves = [
         (0, c.first * HD, int(way), None, c.visit_at * HD, c.heads * HD)
-        for way in (True, False)
+        for way in (False, True)
         for c in by_way[way]
     ]
-    widths = [sum(c.heads for c in by_way[bool(i)]) * HD for i in range(2)]
-    mine = gather(moves, [queries], [(rows, w) for w in widths])
+    widths = [sum(c.heads for c in by_way[way]) * HD for way in (False, True)]
+    mine = gather(
+        moves + key_moves(first, 2, 1),
+        [queries, *keyed],
+        [(rows, w) for w in widths] + key_shapes(first),
+    )
+    mine, packed = mine[:2], mine[2:]
+    packed += gather(key_moves(rest, 0, 0), keyed, key_shapes(rest), after=packed[:1])
     visiting = {}
     for way in (False, True):
         visiting[way] = [mine[int(way)]] + [
             lax.ppermute(mine[int(way)], "reg", pairs_of(count, v, not way, shape))
             for v in range(1, by_way[way][0].sizes(shape)[0])
         ]
-    moves = [
-        (a, c.first * HD, i, a, 0, c.heads * HD) for i, c in enumerate(chunks) for a in range(4)
-    ]
-    packed = gather(
-        moves,
-        [keys_now, values_now, keys_stale, values_stale],
-        [(4, rows, c.heads * HD) for c in chunks],
-        after=mine,
-    )
     shared = {}
     for chunk, pack in zip(chunks, packed):
         shared[chunk] = [pack] + [
@@ -365,36 +379,36 @@
             results[chunk] = [in_vmem(x) for x in kept]
 
     merged, starts = [], []
-    for stage in stages[:-1]:
-        operands = [x for c in stage for x in results[c]]
-        merged.append(
-            pl.pallas_call(
-                functools.partial(
-                    early_merge_kernel, stage, [c.sizes(shape)[0] for c in stage], rows
-                ),
-                in_specs=[vmem] * len(operands),
-                out_specs=vmem,
-                out_shape=result((rows, sum(c.heads for c in stage) * HD), jnp.bfloat16),
-                compiler_params=params,
+    groups = [*stages[:-1], stages[-1][:1], stages[-1][1:]]
+    for group in groups[:-1]:
+        operands = [x for c in group for x in results[c]]
+        merge = pl.pallas_call(
+            functools.partial(
+                early_merge_kernel, group, [c.sizes(shape)[0] for c in group], rows
+            ),
+            in_specs=[vmem] * len(operands),
+            out_specs=vmem,
+            out_shape=result((rows, sum(c.heads for c in group) * HD), jnp.bfloat16),
+            compiler_params=params,
             name="merge",
-            )(*operands)
-        )
-        starts.append(min(c.first for c in stage) * HD)
-    stage = stages[-1]
-    operands = [x for c in stage for x in results[c]]
+        )
+        merged.append(merge(*operands))
+        starts.append(min(c.first for c in group) * HD)
+    group = groups[-1]
+    operands = [x for c in group for x in results[c]]
     return pl.pallas_call(
         functools.partial(
-            last_merge_kernel, stage, [c.sizes(shape)[0] for c in stage], rows, starts
+            last_merge_kernel, group, [c.sizes(shape)[0] for c in group], rows, starts
         ),
         in_specs=[vmem] * (len(merged) + len(operands)),
         out_specs=in_hbm,
         out_shape=jax.ShapeDtypeStruct((rows, width), jnp.bfloat16),
         scratch_shapes=[
-            pltpu.VMEM((rows, sum(c.heads for c in stage) * HD), jnp.bfloat16),
-            pltpu.SemaphoreType.DMA((len(stages),)),
+            pltpu.VMEM((rows, sum(c.heads for c in group) * HD), jnp.bfloat16),
+            pltpu.SemaphoreType.DMA((len(groups),)),
         ],
         compiler_params=params,
-            name="finish",
+        name="finish",
     )(*[in_vmem(x) for x in merged], *operands)
 
 

time: 39 us -> 39.9 us (1.023)
  waiting for transfers between devices: 9 us -> 12.8 us
  starting transfers between devices: 19.3 us -> 16.5 us
  Pallas kernels: 10.4 us -> 9.62 us
  local copies, waits for them, and re-layouts: 0.01 us -> 0.61 us
    ppermute x6, starting transfers between devices: 10.1 us -> 7.23 us  [on_device(): lax.ppermute(pack, 'reg', pairs_of(count, s, chunk.across, shape))]
    ppermute x6, waiting for transfers between devices: 0.23 us -> 2.74 us  [on_device(): lax.ppermute(pack, 'reg', pairs_of(count, s, chunk.across, shape))]
    ppermute x2, waiting for transfers between devices: 5.82 us -> 7.24 us  [on_device(): lax.ppermute(mine[int(way)], 'reg', pairs_of(count, v, not way, shape))]
    pallas_call x6, Pallas kernels: 5.15 us -> 4.14 us  [on_device(): pl.pallas_call(functools.partial(attend_kernel, stage, [blocks[c] for c i...]
    unnamed x2, local copies, waits for them, and re-layouts: 0.01 us -> 0.61 us
    pallas_call x3 -> x4, Pallas kernels: 1.94 us -> 2.16 us  [the longest x3 1.16 us: on_device(): merged.append(merge(*operands))]
  transfers between devices with their start and end apart: 14 -> 14, of which waited for: 5 -> 5; matrix products, arithmetic and copies ran while one was open for 0% -> 0% of each run, Pallas kernels for 17% -> 15%
where the time goes in v2:
time: 39.9 us; the launch traced here: 39.6 us
  starting transfers between devices  16.5 us (41%)
  waiting for transfers between devices  12.8 us (32%)
  Pallas kernels  9.62 us (24%)
  local copies, waits for them, and re-layouts  0.61 us (2%)
    ppermute x2, waiting for transfers between devices, on_device(): lax.ppermute(mine[int(way)], 'reg', pairs_of(count, v, not way, shape))  7.24 us
    ppermute x6, starting transfers between devices, on_device(): lax.ppermute(pack, 'reg', pairs_of(count, s, chunk.across, shape))  7.23 us
    ppermute x6, starting transfers between devices, on_device(): kept.append(lax.ppermute(outs.pop(0), 'reg', pairs))  7.22 us
    pallas_call x6, Pallas kernels, on_device(): pl.pallas_call(functools.partial(attend_kernel, stage, [blocks[c] for c i...  4.14 us
    ppermute x6, waiting for transfers between devices, on_device(): kept.append(lax.ppermute(outs.pop(0), 'reg', pairs))  2.82 us
    ppermute x6, waiting for transfers between devices, on_device(): lax.ppermute(pack, 'reg', pairs_of(count, s, chunk.across, shape))  2.74 us
    pallas_call x2, Pallas kernels, gather(): pl.pallas_call(functools.partial(gather_kernel, moves, len(after)), in_sp...  2.72 us
    ppermute x2, starting transfers between devices, on_device(): lax.ppermute(mine[int(way)], 'reg', pairs_of(count, v, not way, shape))  2.05 us
  transfers between devices with their start and end apart: 14, of which 5 were waited for; matrix products, arithmetic and copies ran while one was open for 0% of the time, Pallas kernels for 15%

profile of v2, /device:TPU:0, one launch (start us, length us, event | category | flops | bytes accessed | tf_op | source)
XLA Modules:
  0.0 39.6 jit_solution(11554273030981061585)
XLA Ops:
  0.0 1.3 %gather.2 = (bf16[128,768]{1,0:T(8,128)(2,1)S(1)}, bf16[128,768]{1,0:T(8,128)(2,1)S(1)}, bf16[4,128,256]{2,1,0:T(8,128)(2,1)S(1)}, bf16[4,128,256]{2,1,0:T(8,128)(2,1)S(1)}) custom-call(bf16[128,1536]{1,0:T(8,128)(2,1)} %refs_0_.1, bf16[128,1536]{1,0:T(8,128)(2,1)} %refs_1_.3, bf16[128,1536]{1,0:T(8,128)(2,1)} %refs_2_.3, bf16[128,1536]{1,0:T(8,128)(2,1)} %refs_3_.3, ...), custom_call_target="tpu_custom_call" | custom-call | tf_op jit(solution)/shard_map/gather/pallas_call | solution.py:288
  1.3 1.4 %gather.3 = (bf16[4,128,256]{2,1,0:T(8,128)(2,1)S(1)}, bf16[4,128,256]{2,1,0:T(8,128)(2,1)S(1)}, bf16[4,128,256]{2,1,0:T(8,128)(2,1)S(1)}, bf16[4,128,256]{2,1,0:T(8,128)(2,1)S(1)}) custom-call(bf16[4,128,256]{2,1,0:T(8,128)(2,1)S(1)} %get-tuple-element.32.refs_3_.refs_0_, bf16[128,1536]{1,0:T(8,128)(2,1)} %refs_1_.3, bf16[128,1536]{1,0:T(8,128)(2,1)} %refs_2_.3, ...), custom_call_target="tpu_custom_call" | custom-call | tf_op jit(solution)/shard_map/gather/pallas_call | solution.py:288
  2.7 3.0 %collective-permute-start.10 = (bf16[4,128,256]{2,1,0:T(8,128)(2,1)S(1)}, bf16[4,128,256]{2,1,0:T(8,128)(2,1)S(1)}, u32[]{:S(2)}, u32[]{:S(2)}) collective-permute-start(bf16[4,128,256]{2,1,0:T(8,128)(2,1)S(1)} %get-tuple-element.49.refs_3_), channel_id=1, source_target_pairs={{1,0},{0,1},{3,2},{2,3},{5,4},{4,5},{7,6},{6,7},{9,8},{8,9},{11,10... | collective-permute-start | bytes 786440 | tf_op jit(solution)/shard_map/ppermute | solution.py:337
  5.8 1.5 %collective-permute-start = (bf16[128,768]{1,0:T(8,128)(2,1)S(1)}, bf16[128,768]{1,0:T(8,128)(2,1)S(1)}, u32[]{:S(2)}, u32[]{:S(2)}) collective-permute-start(bf16[128,768]{1,0:T(8,128)(2,1)S(1)} %get-tuple-element.31.refs_1_), channel_id=1, source_target_pairs={{2,0},{3,1},{0,2},{1,3},{6,4},{7,5},{4,6},{5,7},{10,8},{11,9},{8,1... | collective-permute-start | bytes 589832 | tf_op jit(solution)/shard_map/ppermute | solution.py:331
  7.3 0.5 %collective-permute-start.3 = (bf16[128,768]{1,0:T(8,128)(2,1)S(1)}, bf16[128,768]{1,0:T(8,128)(2,1)S(1)}, u32[]{:S(2)}, u32[]{:S(2)}) collective-permute-start(bf16[128,768]{1,0:T(8,128)(2,1)S(1)} %get-tuple-element.36.refs_1_), channel_id=1, source_target_pairs={{1,0},{0,1},{3,2},{2,3},{5,4},{4,5},{7,6},{6,7},{9,8},{8,9},{11,10... | collective-permute-start | bytes 589832 | tf_op jit(solution)/shard_map/ppermute | solution.py:331
  7.8 0.1 collective-permute-start.4
  7.9 1.9 %collective-permute-start.1 = (bf16[4,128,256]{2,1,0:T(8,128)(2,1)S(1)}, bf16[4,128,256]{2,1,0:T(8,128)(2,1)S(1)}, u32[]{:S(2)}, u32[]{:S(2)}) collective-permute-start(bf16[4,128,256]{2,1,0:T(8,128)(2,1)S(1)} %get-tuple-element.32.refs_3_.refs_0_), channel_id=1, source_target_pairs={{1,0},{0,1},{3,2},{2,3},{5,4},{4,5},{7,6},{6,7},{9,8},{8,9},{11,10... | collective-permute-start | bytes 786440 | tf_op jit(solution)/shard_map/ppermute | solution.py:337
  9.8 3.7 %collective-permute-done.refs_2_ = bf16[128,768]{1,0:T(8,128)(2,1)S(1)} collective-permute-done((bf16[128,768]{1,0:T(8,128)(2,1)S(1)}, bf16[128,768]{1,0:T(8,128)(2,1)S(1)}, u32[]{:S(2)}, u32[]{:S(2)}) %collective-permute-start) | collective-permute-done | bytes 196640 | tf_op jit(solution)/shard_map/ppermute | solution.py:331
  13.5 0.1 collective-permute-start.6
  13.6 3.5 %collective-permute-done.3.refs_2_ = bf16[128,768]{1,0:T(8,128)(2,1)S(1)} collective-permute-done((bf16[128,768]{1,0:T(8,128)(2,1)S(1)}, bf16[128,768]{1,0:T(8,128)(2,1)S(1)}, u32[]{:S(2)}, u32[]{:S(2)}) %collective-permute-start.3) | collective-permute-done | bytes 196640 | tf_op jit(solution)/shard_map/ppermute | solution.py:331
  17.1 2.0 %collective-permute-start.8 = (bf16[4,128,256]{2,1,0:T(8,128)(2,1)S(1)}, bf16[4,128,256]{2,1,0:T(8,128)(2,1)S(1)}, u32[]{:S(2)}, u32[]{:S(2)}) collective-permute-start(bf16[4,128,256]{2,1,0:T(8,128)(2,1)S(1)} %get-tuple-element.45.refs_3_), channel_id=1, source_target_pairs={{2,0},{3,1},{0,2},{1,3},{6,4},{7,5},{4,6},{5,7},{10,8},{11,9},{8,1... | collective-permute-start | bytes 786440 | tf_op jit(solution)/shard_map/ppermute | solution.py:337
  19.2 0.0 collective-permute-done.10.refs_4_
  19.2 0.0 copy-start
  19.2 0.1 collective-permute-start.12
  19.3 0.6 %copy-done = s32[4,2]{0,1:T(2,128)S(1)} copy-done((s32[4,2]{0,1:T(2,128)S(1)}, s32[4,2]{0,1:T(2,128)}, u32[]{:S(2)}) %copy-start) | copy-done | bytes 56
  19.9 0.6 %table.1.refs_0_ = f32[16,128]{1,0:T(8,128)S(1)} custom-call(s32[2,4]{1,0:T(2,128)S(1)} %bitcast.1), custom_call_target="tpu_custom_call" | custom-call | tf_op jit(solution)/shard_map/table/pallas_call | solution.py:343
  20.5 0.7 %attend.10 = (bf16[128,256]{1,0:T(8,128)(2,1)S(1)}, f32[16,128]{1,0:T(8,128)S(1)}, bf16[272,128]{1,0:T(8,128)(2,1)S(1)}) custom-call(f32[16,128]{1,0:T(8,128)S(1)} %table.1.refs_0_, bf16[128,768]{1,0:T(8,128)(2,1)S(1)} %get-tuple-element.31.refs_1_, bf16[128,768]{1,0:T(8,128)(2,1)S(1)} %collective-permute-done.refs_2_, ...), custom_call_target="tpu_custom_call" | custom-call | tf_op jit(solution)/shard_map/attend/pallas_call | solution.py:365
  21.2 0.0 collective-permute-done.4.refs_4_
  21.2 1.4 %collective-permute-start.11 = (bf16[272,128]{1,0:T(8,128)(2,1)S(1)}, bf16[272,128]{1,0:T(8,128)(2,1)S(1)}, u32[]{:S(2)}, u32[]{:S(2)}) collective-permute-start(bf16[272,128]{1,0:T(8,128)(2,1)S(1)} %get-tuple-element.52), channel_id=1, source_target_pairs={{0,2},{1,3},{2,0},{3,1},{4,6},{5,7},{6,4},{7,5},{8,10},{9,11},{10,... | collective-permute-start | bytes 208904 | tf_op jit(solution)/shard_map/ppermute | solution.py:378
  22.6 0.7 %attend.7 = (bf16[128,256]{1,0:T(8,128)(2,1)S(1)}, f32[16,128]{1,0:T(8,128)S(1)}, bf16[272,128]{1,0:T(8,128)(2,1)S(1)}) custom-call(f32[16,128]{1,0:T(8,128)S(1)} %table.1.refs_0_, bf16[128,768]{1,0:T(8,128)(2,1)S(1)} %get-tuple-element.36.refs_1_, bf16[128,768]{1,0:T(8,128)(2,1)S(1)} %collective-permute-done.3.refs_2_, ...), custom_call_target="tpu_custom_call" | custom-call | tf_op jit(solution)/shard_map/attend/pallas_call | solution.py:365
  23.3 0.0 collective-permute-done.1.refs_4_
  23.3 1.6 %collective-permute-start.5 = (bf16[272,128]{1,0:T(8,128)(2,1)S(1)}, bf16[272,128]{1,0:T(8,128)(2,1)S(1)}, u32[]{:S(2)}, u32[]{:S(2)}) collective-permute-start(bf16[272,128]{1,0:T(8,128)(2,1)S(1)} %get-tuple-element.40), channel_id=1, source_target_pairs={{0,1},{1,0},{2,3},{3,2},{4,5},{5,4},{6,7},{7,6},{8,9},{9,8},{10,11... | collective-permute-start | bytes 208904 | tf_op jit(solution)/shard_map/ppermute | solution.py:378
  24.8 0.7 %attend.6 = (bf16[128,256]{1,0:T(8,128)(2,1)S(1)}, f32[16,128]{1,0:T(8,128)S(1)}, bf16[272,128]{1,0:T(8,128)(2,1)S(1)}) custom-call(f32[16,128]{1,0:T(8,128)S(1)} %table.1.refs_0_, bf16[128,768]{1,0:T(8,128)(2,1)S(1)} %get-tuple-element.31.refs_1_, bf16[128,768]{1,0:T(8,128)(2,1)S(1)} %collective-permute-done.refs_2_, ...), custom_call_target="tpu_custom_call" | custom-call | tf_op jit(solution)/shard_map/attend/pallas_call | solution.py:365
  25.5 2.7 %collective-permute-done.6.refs_4_ = bf16[4,128,256]{2,1,0:T(8,128)(2,1)S(1)} collective-permute-done((bf16[4,128,256]{2,1,0:T(8,128)(2,1)S(1)}, bf16[4,128,256]{2,1,0:T(8,128)(2,1)S(1)}, u32[]{:S(2)}, u32[]{:S(2)}) %collective-permute-start.6) | collective-permute-done | bytes 262176 | tf_op jit(solution)/shard_map/ppermute | solution.py:337
  28.3 1.8 %collective-permute-start.2 = (bf16[272,128]{1,0:T(8,128)(2,1)S(1)}, bf16[272,128]{1,0:T(8,128)(2,1)S(1)}, u32[]{:S(2)}, u32[]{:S(2)}) collective-permute-start(bf16[272,128]{1,0:T(8,128)(2,1)S(1)} %get-tuple-element.35), channel_id=1, source_target_pairs={{0,2},{1,3},{2,0},{3,1},{4,6},{5,7},{6,4},{7,5},{8,10},{9,11},{10,... | collective-permute-start | bytes 208904 | tf_op jit(solution)/shard_map/ppermute | solution.py:378
  30.0 0.7 %attend.8 = (bf16[128,256]{1,0:T(8,128)(2,1)S(1)}, f32[16,128]{1,0:T(8,128)S(1)}, bf16[272,128]{1,0:T(8,128)(2,1)S(1)}) custom-call(f32[16,128]{1,0:T(8,128)S(1)} %table.1.refs_0_, bf16[128,768]{1,0:T(8,128)(2,1)S(1)} %get-tuple-element.31.refs_1_, bf16[128,768]{1,0:T(8,128)(2,1)S(1)} %collective-permute-done.refs_2_, ...), custom_call_target="tpu_custom_call" | custom-call | tf_op jit(solution)/shard_map/attend/pallas_call | solution.py:365
  30.7 0.0 collective-permute-done.8.refs_4_
  30.7 0.3 collective-permute-start.7
  31.1 0.7 %attend.9 = (bf16[128,256]{1,0:T(8,128)(2,1)S(1)}, f32[16,128]{1,0:T(8,128)S(1)}, bf16[272,128]{1,0:T(8,128)(2,1)S(1)}) custom-call(f32[16,128]{1,0:T(8,128)S(1)} %table.1.refs_0_, bf16[128,768]{1,0:T(8,128)(2,1)S(1)} %get-tuple-element.36.refs_1_, bf16[128,768]{1,0:T(8,128)(2,1)S(1)} %collective-permute-done.3.refs_2_, ...), custom_call_target="tpu_custom_call" | custom-call | tf_op jit(solution)/shard_map/attend/pallas_call | solution.py:365
  31.8 0.0 collective-permute-done.12.refs_4_
  31.8 1.8 %collective-permute-start.9 = (bf16[272,128]{1,0:T(8,128)(2,1)S(1)}, bf16[272,128]{1,0:T(8,128)(2,1)S(1)}, u32[]{:S(2)}, u32[]{:S(2)}) collective-permute-start(bf16[272,128]{1,0:T(8,128)(2,1)S(1)} %get-tuple-element.48), channel_id=1, source_target_pairs={{0,1},{1,0},{2,3},{3,2},{4,5},{5,4},{6,7},{7,6},{8,9},{9,8},{10,11... | collective-permute-start | bytes 208904 | tf_op jit(solution)/shard_map/ppermute | solution.py:378
  33.6 0.7 %attend.11 = (bf16[128,256]{1,0:T(8,128)(2,1)S(1)}, f32[16,128]{1,0:T(8,128)S(1)}, bf16[272,128]{1,0:T(8,128)(2,1)S(1)}) custom-call(f32[16,128]{1,0:T(8,128)S(1)} %table.1.refs_0_, bf16[128,768]{1,0:T(8,128)(2,1)S(1)} %get-tuple-element.36.refs_1_, bf16[128,768]{1,0:T(8,128)(2,1)S(1)} %collective-permute-done.3.refs_2_, ...), custom_call_target="tpu_custom_call" | custom-call | tf_op jit(solution)/shard_map/attend/pallas_call | solution.py:365
  34.3 0.0 collective-permute-done.11.refs_2_
  34.3 0.4 collective-permute-start.13
  34.6 0.3 merge.5.refs_2_
  34.9 0.0 collective-permute-done.5.refs_5_
  35.0 0.0 collective-permute-done.2.refs_2_
  35.0 0.4 %merge.3.refs_0_ = bf16[128,512]{1,0:T(8,128)(2,1)S(1)} custom-call(bf16[128,256]{1,0:T(8,128)(2,1)S(1)} %get-tuple-element.33.refs_0_, f32[16,128]{1,0:T(8,128)S(1)} %get-tuple-element.34.refs_1_, bf16[272,128]{1,0:T(8,128)(2,1)S(1)} %collective-permute-done.2.refs_2_, bf16[128,256]{1,0:T(8,128)(2,1)S(1)} %get-tuple-element.38.refs_3_, ...), custom_call_target="tpu_custom_call" | custom-call | tf_op jit(solution)/shard_map/merge/pallas_call | solution.py:395
  35.4 0.0 collective-permute-done.7.refs_2_
  35.4 0.7 %collective-permute-done.9.refs_5_ = bf16[272,128]{1,0:T(8,128)(2,1)S(1)} collective-permute-done((bf16[272,128]{1,0:T(8,128)(2,1)S(1)}, bf16[272,128]{1,0:T(8,128)(2,1)S(1)}, u32[]{:S(2)}, u32[]{:S(2)}) %collective-permute-start.9) | collective-permute-done | bytes 69664 | tf_op jit(solution)/shard_map/ppermute | solution.py:378
  36.1 0.4 %merge.4.refs_1_ = bf16[128,512]{1,0:T(8,128)(2,1)S(1)} custom-call(bf16[128,256]{1,0:T(8,128)(2,1)S(1)} %get-tuple-element.42.refs_0_, f32[16,128]{1,0:T(8,128)S(1)} %get-tuple-element.43.refs_1_, bf16[272,128]{1,0:T(8,128)(2,1)S(1)} %collective-permute-done.7.refs_2_, bf16[128,256]{1,0:T(8,128)(2,1)S(1)} %get-tuple-element.46.refs_3_, ...), custom_call_target="tpu_custom_call" | custom-call | tf_op jit(solution)/shard_map/merge/pallas_call | solution.py:395
  36.6 2.1 %collective-permute-done.13.refs_5_ = bf16[272,128]{1,0:T(8,128)(2,1)S(1)} collective-permute-done((bf16[272,128]{1,0:T(8,128)(2,1)S(1)}, bf16[272,128]{1,0:T(8,128)(2,1)S(1)}, u32[]{:S(2)}, u32[]{:S(2)}) %collective-permute-start.13) | collective-permute-done | bytes 69664 | tf_op jit(solution)/shard_map/ppermute | solution.py:378
  38.6 1.0 %finish.1 = bf16[128,1536]{1,0:T(8,128)(2,1)} custom-call(bf16[128,512]{1,0:T(8,128)(2,1)S(1)} %merge.3.refs_0_, bf16[128,512]{1,0:T(8,128)(2,1)S(1)} %merge.4.refs_1_, bf16[128,256]{1,0:T(8,128)(2,1)S(1)} %merge.5.refs_2_, bf16[128,256]{1,0:T(8,128)(2,1)S(1)} %get-tuple-element.54.refs_3_, f32[16,128]{1,0:T(8,128)S(1)} %get-tuple-element.55.refs_4_, ...), custom_call_target="tpu_custom_call" | custom-call | tf_op jit(solution)/shard_map/finish/pallas_call | solution.py:399
Async XLA Ops:
  2.7 16.5 %collective-permute-start.10 = (bf16[4,128,256]{2,1,0:T(8,128)(2,1)S(1)}, bf16[4,128,256]{2,1,0:T(8,128)(2,1)S(1)}, u32[]{:S(2)}, u32[]{:S(2)}) collective-permute-start(bf16[4,128,256]{2,1,0:T(8,128)(2,1)S(1)} %get-tuple-element.49.refs_3_), channel_id=1, source_target_pairs={{1,0},{0,1},{3,2},{2,3},{5,4},{4,5},{7,6},{6,7},{9,8},{8,9},{11,10... | collective-permute-start | bytes 786440 | tf_op jit(solution)/shard_map/ppermute | solution.py:337
  5.8 7.8 %collective-permute-start = (bf16[128,768]{1,0:T(8,128)(2,1)S(1)}, bf16[128,768]{1,0:T(8,128)(2,1)S(1)}, u32[]{:S(2)}, u32[]{:S(2)}) collective-permute-start(bf16[128,768]{1,0:T(8,128)(2,1)S(1)} %get-tuple-element.31.refs_1_), channel_id=1, source_target_pairs={{2,0},{3,1},{0,2},{1,3},{6,4},{7,5},{4,6},{5,7},{10,8},{11,9},{8,1... | collective-permute-start | bytes 589832 | tf_op jit(solution)/shard_map/ppermute | solution.py:331
  7.3 9.8 %collective-permute-start.3 = (bf16[128,768]{1,0:T(8,128)(2,1)S(1)}, bf16[128,768]{1,0:T(8,128)(2,1)S(1)}, u32[]{:S(2)}, u32[]{:S(2)}) collective-permute-start(bf16[128,768]{1,0:T(8,128)(2,1)S(1)} %get-tuple-element.36.refs_1_), channel_id=1, source_target_pairs={{1,0},{0,1},{3,2},{2,3},{5,4},{4,5},{7,6},{6,7},{9,8},{8,9},{11,10... | collective-permute-start | bytes 589832 | tf_op jit(solution)/shard_map/ppermute | solution.py:331
  7.8 13.3 %collective-permute-start.4 = (bf16[4,128,256]{2,1,0:T(8,128)(2,1)S(1)}, bf16[4,128,256]{2,1,0:T(8,128)(2,1)S(1)}, u32[]{:S(2)}, u32[]{:S(2)}) collective-permute-start(bf16[4,128,256]{2,1,0:T(8,128)(2,1)S(1)} %get-tuple-element.37.refs_3_), channel_id=1, source_target_pairs={{2,0},{3,1},{0,2},{1,3},{6,4},{7,5},{4,6},{5,7},{10,8},{11,9},{8,1... | collective-permute-start | bytes 786440 | tf_op jit(solution)/shard_map/ppermute | solution.py:337
  7.9 15.4 %collective-permute-start.1 = (bf16[4,128,256]{2,1,0:T(8,128)(2,1)S(1)}, bf16[4,128,256]{2,1,0:T(8,128)(2,1)S(1)}, u32[]{:S(2)}, u32[]{:S(2)}) collective-permute-start(bf16[4,128,256]{2,1,0:T(8,128)(2,1)S(1)} %get-tuple-element.32.refs_3_.refs_0_), channel_id=1, source_target_pairs={{1,0},{0,1},{3,2},{2,3},{5,4},{4,5},{7,6},{6,7},{9,8},{8,9},{11,10... | collective-permute-start | bytes 786440 | tf_op jit(solution)/shard_map/ppermute | solution.py:337
  13.5 14.7 %collective-permute-start.6 = (bf16[4,128,256]{2,1,0:T(8,128)(2,1)S(1)}, bf16[4,128,256]{2,1,0:T(8,128)(2,1)S(1)}, u32[]{:S(2)}, u32[]{:S(2)}) collective-permute-start(bf16[4,128,256]{2,1,0:T(8,128)(2,1)S(1)} %get-tuple-element.41.refs_3_), channel_id=1, source_target_pairs={{1,0},{0,1},{3,2},{2,3},{5,4},{4,5},{7,6},{6,7},{9,8},{8,9},{11,10... | collective-permute-start | bytes 786440 | tf_op jit(solution)/shard_map/ppermute | solution.py:337
  17.1 13.6 %collective-permute-start.8 = (bf16[4,128,256]{2,1,0:T(8,128)(2,1)S(1)}, bf16[4,128,256]{2,1,0:T(8,128)(2,1)S(1)}, u32[]{:S(2)}, u32[]{:S(2)}) collective-permute-start(bf16[4,128,256]{2,1,0:T(8,128)(2,1)S(1)} %get-tuple-element.45.refs_3_), channel_id=1, source_target_pairs={{2,0},{3,1},{0,2},{1,3},{6,4},{7,5},{4,6},{5,7},{10,8},{11,9},{8,1... | collective-permute-start | bytes 786440 | tf_op jit(solution)/shard_map/ppermute | solution.py:337
  19.2 0.7 %copy-start = (s32[4,2]{0,1:T(2,128)S(1)}, s32[4,2]{0,1:T(2,128)}, u32[]{:S(2)}) copy-start(s32[4,2]{0,1:T(2,128)} %param.11) | copy-start | bytes 100
  19.2 12.6 %collective-permute-start.12 = (bf16[4,128,256]{2,1,0:T(8,128)(2,1)S(1)}, bf16[4,128,256]{2,1,0:T(8,128)(2,1)S(1)}, u32[]{:S(2)}, u32[]{:S(2)}) collective-permute-start(bf16[4,128,256]{2,1,0:T(8,128)(2,1)S(1)} %get-tuple-element.53.refs_3_), channel_id=1, source_target_pairs={{2,0},{3,1},{0,2},{1,3},{6,4},{7,5},{4,6},{5,7},{10,8},{11,9},{8,1... | collective-permute-start | bytes 786440 | tf_op jit(solution)/shard_map/ppermute | solution.py:337
  21.2 13.1 %collective-permute-start.11 = (bf16[272,128]{1,0:T(8,128)(2,1)S(1)}, bf16[272,128]{1,0:T(8,128)(2,1)S(1)}, u32[]{:S(2)}, u32[]{:S(2)}) collective-permute-start(bf16[272,128]{1,0:T(8,128)(2,1)S(1)} %get-tuple-element.52), channel_id=1, source_target_pairs={{0,2},{1,3},{2,0},{3,1},{4,6},{5,7},{6,4},{7,5},{8,10},{9,11},{10,... | collective-permute-start | bytes 208904 | tf_op jit(solution)/shard_map/ppermute | solution.py:378
  23.3 11.7 %collective-permute-start.5 = (bf16[272,128]{1,0:T(8,128)(2,1)S(1)}, bf16[272,128]{1,0:T(8,128)(2,1)S(1)}, u32[]{:S(2)}, u32[]{:S(2)}) collective-permute-start(bf16[272,128]{1,0:T(8,128)(2,1)S(1)} %get-tuple-element.40), channel_id=1, source_target_pairs={{0,1},{1,0},{2,3},{3,2},{4,5},{5,4},{6,7},{7,6},{8,9},{9,8},{10,11... | collective-permute-start | bytes 208904 | tf_op jit(solution)/shard_map/ppermute | solution.py:378
  28.3 6.7 %collective-permute-start.2 = (bf16[272,128]{1,0:T(8,128)(2,1)S(1)}, bf16[272,128]{1,0:T(8,128)(2,1)S(1)}, u32[]{:S(2)}, u32[]{:S(2)}) collective-permute-start(bf16[272,128]{1,0:T(8,128)(2,1)S(1)} %get-tuple-element.35), channel_id=1, source_target_pairs={{0,2},{1,3},{2,0},{3,1},{4,6},{5,7},{6,4},{7,5},{8,10},{9,11},{10,... | collective-permute-start | bytes 208904 | tf_op jit(solution)/shard_map/ppermute | solution.py:378
  30.7 4.6 %collective-permute-start.7 = (bf16[272,128]{1,0:T(8,128)(2,1)S(1)}, bf16[272,128]{1,0:T(8,128)(2,1)S(1)}, u32[]{:S(2)}, u32[]{:S(2)}) collective-permute-start(bf16[272,128]{1,0:T(8,128)(2,1)S(1)} %get-tuple-element.44), channel_id=1, source_target_pairs={{0,2},{1,3},{2,0},{3,1},{4,6},{5,7},{6,4},{7,5},{8,10},{9,11},{10,... | collective-permute-start | bytes 208904 | tf_op jit(solution)/shard_map/ppermute | solution.py:378
  31.8 4.4 %collective-permute-start.9 = (bf16[272,128]{1,0:T(8,128)(2,1)S(1)}, bf16[272,128]{1,0:T(8,128)(2,1)S(1)}, u32[]{:S(2)}, u32[]{:S(2)}) collective-permute-start(bf16[272,128]{1,0:T(8,128)(2,1)S(1)} %get-tuple-element.48), channel_id=1, source_target_pairs={{0,1},{1,0},{2,3},{3,2},{4,5},{5,4},{6,7},{7,6},{8,9},{9,8},{10,11... | collective-permute-start | bytes 208904 | tf_op jit(solution)/shard_map/ppermute | solution.py:378
  34.3 4.4 %collective-permute-start.13 = (bf16[272,128]{1,0:T(8,128)(2,1)S(1)}, bf16[272,128]{1,0:T(8,128)(2,1)S(1)}, u32[]{:S(2)}, u32[]{:S(2)}) collective-permute-start(bf16[272,128]{1,0:T(8,128)(2,1)S(1)} %get-tuple-element.56), channel_id=1, source_target_pairs={{0,1},{1,0},{2,3},{3,2},{4,5},{5,4},{6,7},{7,6},{8,9},{9,8},{10,11... | collective-permute-start | bytes 208904 | tf_op jit(solution)/shard_map/ppermute | solution.py:378
